TPU v7x, 768 devices: a whole 4x8x12 slice. The times are simulated.
768 devices in a mesh: users: 48 (over z_hi, y, core), items: 16 (over x, z_lo).
Axes of the slice: x: 4, y: 8, z: 12 (z_hi: 3, z_lo: 4; z = z_hi * 4 + z_lo), core: 2. Of those that a mesh axis runs over, the one named last changes fastest.
Arguments:
- user_factors: float32 [98304, 128], P('users'), may hold values from -1.8 to 1.8
- user_moment_one: float32 [98304, 128], P('users'), may hold values from -1.8 to 1.8
- user_moment_two: float32 [98304, 128], P('users'), may hold values from 0.01 to 1
- item_factors: float32 [24576, 128], P(('items', 'users')), may hold values from -1.8 to 1.8
- item_moment_one: float32 [24576, 128], P(('items', 'users')), may hold values from -1.8 to 1.8
- item_moment_two: float32 [24576, 128], P(('items', 'users')), may hold values from 0.01 to 1
- block_slot: int32 [48, 16, 128], P('users', 'items'), may hold values from 0 to 191, as said below
- block_count: int32 [48, 16], P('users', 'items'), may hold values from 32 to 128, as said below
- block_values: bfloat16 [48, 16, 128, 128, 128], P('users', 'items'), may hold values from 0 to 4
Outputs:
- new_user_factors: float32 [98304, 128], P(('users', 'items'))
- new_user_moment_one: float32 [98304, 128], P(('users', 'items'))
- new_user_moment_two: float32 [98304, 128], P(('users', 'items'))
- new_item_factors: float32 [24576, 128], P(('items', 'users'))
- new_item_moment_one: float32 [24576, 128], P(('items', 'users'))
- new_item_moment_two: float32 [24576, 128], P(('items', 'users'))
Inputs may be any that keep to these rules, and one draw needn't show every extreme that they name: `block_slot`: in every grid cell the 128 entries are distinct. `block_count`: some grid cell has exactly 128 live blocks.
All inputs are finite; a program needn't handle non-finite values.
Results may differ from a plain program's by a relative error of at most 0.0046.
Values may be sent and summed in bfloat16 or wider, within the bound.
No kernel may reach another device: no remote copies, remote signals or barrier semaphores. Data moves between devices by JAX's collectives and lax.ppermute only.
A program may use at most 64 MiB of HBM per device.

v0:
```python
import math

import jax
import jax.numpy as jnp
from jax import lax
from jax.sharding import PartitionSpec as P

conf_alpha = 0.5
reg_weight = 0.5
beta_one = 0.9
beta_two = 0.95
learn_rate = 0.1
adam_eps = 1e-08
correction_one = 1.0 - beta_one**11
correction_two = 1.0 - beta_two**11


def adam_update(parameter, first_moment, second_moment, grad_sum, grad_scale):
    gradient = grad_sum * grad_scale + reg_weight * parameter
    first_new = beta_one * first_moment + (1.0 - beta_one) * gradient
    second_new = beta_two * second_moment + (1.0 - beta_two) * gradient * gradient
    step_size = first_new / correction_one / (jnp.sqrt(second_new / correction_two) + adam_eps)
    return (parameter - learn_rate * step_size, first_new, second_new)


def weighted_error(predicted, block_vals, live_mask):
    target = block_vals.astype(jnp.float32)
    return jnp.where(live_mask, (1.0 + conf_alpha * target) * (predicted - target), 0.0).astype(
        jnp.bfloat16
    )


def listed_pass(user_panel, item_panel, slot_list, live_count, block_vals, toward_users):
    capacity = slot_list.shape[0]
    group_size = math.gcd(8, capacity)
    item_blocks = item_panel.shape[0]
    user_block = slot_list // item_blocks
    item_block = slot_list % item_blocks
    if toward_users:
        running = jnp.zeros(user_panel.shape, jnp.float32)
    else:
        running = jnp.zeros(item_panel.shape, jnp.float32)

    def advance(turn_number, running):
        first_row = turn_number * group_size
        user_part = lax.dynamic_slice_in_dim(user_block, first_row, group_size)
        item_part = lax.dynamic_slice_in_dim(item_block, first_row, group_size)
        these_values = lax.dynamic_slice_in_dim(block_vals, first_row, group_size)
        live_mask = first_row + jnp.arange(group_size, dtype=jnp.int32) < live_count
        user_rows = user_panel[user_part]
        item_rows = item_panel[item_part]
        predicted = jnp.einsum(
            "kar,kbr->kab", user_rows, item_rows, preferred_element_type=jnp.float32
        )
        weighted = weighted_error(predicted, these_values, live_mask[:, None, None])
        if toward_users:
            return running.at[user_part].add(
                jnp.einsum("kab,kbr->kar", weighted, item_rows, preferred_element_type=jnp.float32)
            )
        return running.at[item_part].add(
            jnp.einsum("kab,kar->kbr", weighted, user_rows, preferred_element_type=jnp.float32)
        )

    return lax.fori_loop(0, (live_count + group_size - 1) // group_size, advance, running)


def on_device(
    user_factors,
    user_moment_one,
    user_moment_two,
    item_factors,
    item_moment_one,
    item_moment_two,
    block_slot,
    block_count,
    block_values,
):
    slot_list = block_slot[0, 0]
    live_count = block_count[0, 0]
    values_here = block_values[0, 0]
    rank = user_factors.shape[1]
    block_edge = values_here.shape[-1]
    gathered = lax.all_gather(item_factors.astype(jnp.bfloat16), "users", axis=0, tiled=True)
    item_panel = gathered.reshape(-1, block_edge, rank)
    user_panel = user_factors.astype(jnp.bfloat16).reshape(-1, block_edge, rank)
    item_total = item_panel.shape[0] * block_edge * lax.axis_size("items")
    user_total = user_factors.shape[0] * lax.axis_size("users")
    user_partial = listed_pass(user_panel, item_panel, slot_list, live_count, values_here, True)
    user_partial = user_partial.reshape(-1, rank)
    user_share = user_factors.shape[0] // lax.axis_size("items")
    user_offset = lax.axis_index("items") * user_share
    user_sum = lax.psum(user_partial, "items")
    new_user, new_user_one, new_user_two = adam_update(
        user_factors, user_moment_one, user_moment_two, user_sum, 1.0 / math.sqrt(item_total)
    )
    new_low = new_user.astype(jnp.bfloat16)
    new_user = lax.dynamic_slice_in_dim(new_user, user_offset, user_share, 0)
    new_user_one = lax.dynamic_slice_in_dim(new_user_one, user_offset, user_share, 0)
    new_user_two = lax.dynamic_slice_in_dim(new_user_two, user_offset, user_share, 0)
    new_panel = new_low.reshape(-1, block_edge, rank)
    item_partial = listed_pass(new_panel, item_panel, slot_list, live_count, values_here, False)
    item_partial = item_partial.reshape(-1, rank)
    item_whole_sum = lax.psum(item_partial, "users")
    item_share = item_factors.shape[0]
    item_sum = lax.dynamic_slice_in_dim(
        item_whole_sum, lax.axis_index("users") * item_share, item_share, 0
    )
    new_item, new_item_one, new_item_two = adam_update(
        item_factors, item_moment_one, item_moment_two, item_sum, 1.0 / math.sqrt(user_total)
    )
    return (new_user, new_user_one, new_user_two, new_item, new_item_one, new_item_two)


def solution(mesh):
    return jax.shard_map(
        on_device,
        mesh=mesh,
        in_specs=(
            P("users", None),
            P("users", None),
            P("users", None),
            P(("items", "users"), None),
            P(("items", "users"), None),
            P(("items", "users"), None),
            P("users", "items", None),
            P("users", "items"),
            P("users", "items", None, None, None),
        ),
        out_specs=(
            P(("users", "items"), None),
            P(("users", "items"), None),
            P(("users", "items"), None),
            P(("items", "users"), None),
            P(("items", "users"), None),
            P(("items", "users"), None),
        ),
        check_vma=False,
    )
```

profile of v0, /device:TPU:1, one launch (start us, length us, event | category | flops | bytes accessed | tf_op | source)
XLA Modules:
  0.0 932.2 jit_solution(6229361754681963804)
XLA Ops:
  9.3 86.2 %all_gather.3 = bf16[1536,128]{1,0:T(8,128)(2,1)S(1)} all-gather(bf16[32,128]{1,0:T(8,128)(2,1)S(1)} %convert_element_type.22), channel_id=1, replica_groups=mesh['users'=48,'items'=16] {'users'}, dimensions={0}, use_global_device_ids=true | all-gather | bytes 401408 | tf_op jit(solution)/shard_map/all_gather | solution.py:83
  95.4 1.3 convert_element_type.21
  96.8 26.5 %while.20 = (s32[]{:T(128)}, f32[16,128,128]{2,1,0:T(8,128)S(1)}, s32[]{:T(128)}, s32[128]{0:T(128)S(1)}, s32[]{:T(128)}, /*index=5*/bf16[128,128,128]{2,1,0:T(8...) while((s32[]{:T(128)}, f32[16,128,128]{2,1,0:T(8,128)S(1)}, ...), condition=%wide.region_2.3_spmd, body=%wide.region_0.2_spmd.sunk | while | flops 68159560 | bytes 4203491 | solution.py:64
  98.8 1.4 fusion.55
  103.2 1.4 fusion.55
  107.6 1.4 fusion.55
  112.1 1.4 fusion.55
  116.5 1.4 fusion.55
  120.9 1.4 fusion.55
  124.4 6.5 copy.15
  130.9 195.2 %all-reduce.3.cloned.1.call-done = f32[2048,128]{1,0:T(8,128)} async-done(((f32[2048,128]{1,0:T(8,128)}), f32[2048,128]{1,0:T(8,128)}) %all-reduce.3.cloned.1.call-update) | async-done | bytes 1048592 | tf_op jit(solution)/shard_map/psum | solution.py:92
  326.0 4.1 fusion.36
  330.2 26.5 %while.21 = (s32[]{:T(128)}, f32[12,128,128]{2,1,0:T(8,128)S(1)}, s32[]{:T(128)}, s32[128]{0:T(128)S(1)}, s32[]{:T(128)}, /*index=5*/bf16[128,128,128]{1,2,0:T(8...) while((s32[]{:T(128)}, f32[12,128,128]{2,1,0:T(8,128)S(1)}, ...), condition=%wide.region_6.7_spmd, body=%wide.region_4.6_spmd.sunk | while | flops 68159560 | bytes 4203491 | solution.py:64
  332.2 1.4 fusion.59
  336.6 1.4 fusion.59
  338.0 1.0 scatter_fusion.1
  341.0 1.4 fusion.59
  345.4 1.4 fusion.59
  349.9 1.4 fusion.59
  354.3 1.4 fusion.59
  357.6 1.5 constant_dynamic-slice_fusion.2
  359.1 1.5 constant_dynamic-slice_fusion
  360.7 563.4 %all-reduce.5.cloned.1.call-done = f32[1536,128]{1,0:T(8,128)} async-done(((f32[1536,128]{1,0:T(8,128)}), f32[1536,128]{1,0:T(8,128)}) %all-reduce.5.cloned.1.call-update) | async-done | bytes 786448 | tf_op jit(solution)/shard_map/psum | solution.py:103
  924.0 1.4 multiply_subtract_fusion.1
  (103 shorter events, 38.2 us)
Async XLA Ops:
  7.2 318.9 %all-reduce.3.cloned.1.call-start = ((), (), s32[]{:S(2)}) async-start(), calls=%async_computation | async-start | bytes 2097152 | tf_op jit(solution)/shard_map/psum | solution.py:92
  123.3 1.0 copy-start.1
  124.3 799.7 %all-reduce.5.cloned.1.call-start = ((), (), s32[]{:S(2)}) async-start(), calls=%async_computation.1 | async-start | bytes 1572864 | tf_op jit(solution)/shard_map/psum | solution.py:103
  124.4 201.6 %copy-start.2 = (f32[2048,128]{1,0:T(8,128)S(1)}, f32[2048,128]{1,0:T(8,128)}, u32[]{:S(2)}) copy-start(f32[2048,128]{1,0:T(8,128)} %param.13) | copy-start | bytes 3145732
  330.2 593.9 %copy-start.3 = (f32[32,128]{1,0:T(8,128)S(1)}, f32[32,128]{1,0:T(8,128)}, u32[]{:S(2)}) copy-start(f32[32,128]{1,0:T(8,128)} %param.16) | copy-start | bytes 49156
  330.2 593.8 %copy-start.4 = (f32[32,128]{1,0:T(8,128)S(1)}, f32[32,128]{1,0:T(8,128)}, u32[]{:S(2)}) copy-start(f32[32,128]{1,0:T(8,128)} %param.17) | copy-start | bytes 49156
  330.2 593.8 %copy-start.5 = (f32[32,128]{1,0:T(8,128)S(1)}, f32[32,128]{1,0:T(8,128)}, u32[]{:S(2)}) copy-start(f32[32,128]{1,0:T(8,128)} %param.18) | copy-start | bytes 49156
  356.7 0.9 copy-start
Sparse Core Ops, SparseCore 0:
  124.5 201.5 all-reduce.2
  357.8 566.2 all-reduce.4
where the time goes:
time: 934 us; the launch traced here: 932 us
  waiting for transfers between devices  759 us (81%)
  blocking collectives  86.2 us (9%)
  other arithmetic  29.4 us (3%)
  local copies, waits for them, and re-layouts  25.8 us (3%)
  matrix products  16.6 us (2%)
  between operations  14.8 us (2%)
    psum x1, waiting for transfers between devices, on_device(): item_whole_sum = lax.psum(item_partial, 'users')  563 us
    psum x1, waiting for transfers between devices, on_device(): user_sum = lax.psum(user_partial, 'items')  195 us
    all_gather x1, blocking collectives, on_device(): lax.all_gather(item_factors.astype(jnp.bfloat16), 'users', axis=0, tiled=...  86.2 us
  transfers between devices with their start and end apart: 2, of which 2 were waited for; matrix products, arithmetic and copies ran while one was open for 1% of the time, Pallas kernels for 0%

commit v1 on v0

v1 whole, which is shorter than its diff:
```python
import functools
import math

import jax
import jax.numpy as jnp
from jax import lax
from jax.experimental import pallas as pl
from jax.experimental.pallas import tpu as pltpu
from jax.sharding import Mesh
from jax.sharding import PartitionSpec as P

conf_alpha = 0.5
reg_weight = 0.5
beta_one = 0.9
beta_two = 0.95
learn_rate = 0.1
adam_eps = 1e-08
correction_one = 1.0 - beta_one**11
correction_two = 1.0 - beta_two**11

EDGE = 128
RANK = 128
UBLK = 16
IBLK = 12
MAXB = 128
CHUNK = 8
PARTS = ("z_hi", "y", "core", "x", "z_lo")
USERS = PARTS[:3]
ITEMS = PARTS[3:]


def adam_update(parameter, first_moment, second_moment, grad_sum, grad_scale):
    gradient = grad_sum * grad_scale + reg_weight * parameter
    first_new = beta_one * first_moment + (1.0 - beta_one) * gradient
    second_new = beta_two * second_moment + (1.0 - beta_two) * gradient * gradient
    step_size = first_new / correction_one / (jnp.sqrt(second_new / correction_two) + adam_eps)
    return (parameter - learn_rate * step_size, first_new, second_new)


def dot_nt(left, right):
    return lax.dot_general(
        left, right, (((1,), (1,)), ((), ())), preferred_element_type=jnp.float32
    )


def dot_nn(left, right):
    return lax.dot_general(
        left, right, (((1,), (0,)), ((), ())), preferred_element_type=jnp.float32
    )


def load_values(count, values, buffer, arrivals):
    for chunk in range(MAXB // CHUNK):

        @pl.when(chunk * CHUNK < count)
        def _():
            pltpu.make_async_copy(
                values.at[pl.ds(chunk * CHUNK, CHUNK)],
                buffer.at[pl.ds(chunk * CHUNK, CHUNK)],
                arrivals.at[chunk],
            ).start()


def await_values(count, values, buffer, arrivals):
    for chunk in range(MAXB // CHUNK):

        @pl.when(chunk * CHUNK < count)
        def _():
            pltpu.make_async_copy(
                values.at[pl.ds(chunk * CHUNK, CHUNK)],
                buffer.at[pl.ds(chunk * CHUNK, CHUNK)],
                arrivals.at[chunk],
            ).wait()


def fill_places(count, slots, places):
    for place in range(UBLK * IBLK):
        places[place] = MAXB

    def advance(turn, carry):
        for inner in range(CHUNK):
            listed = turn * CHUNK + inner
            place = slots[listed]
            places[place] = jnp.where(listed < count, listed, places[place])
        return carry

    lax.fori_loop(0, (count + CHUNK - 1) // CHUNK, advance, 0)


def weighted(predicted, target):
    target = target.astype(jnp.float32)
    return ((1.0 + conf_alpha * target) * (predicted - target)).astype(jnp.bfloat16)


def square_error(user_pair, item_pair, first_place, places, buffer):
    predicted = dot_nt(user_pair, item_pair)
    rows = []
    for row in range(2):
        columns = []
        for column in range(2):
            block = buffer[places[first_place + row * IBLK + column]]
            columns.append(
                weighted(
                    predicted[row * EDGE : (row + 1) * EDGE, column * EDGE : (column + 1) * EDGE],
                    block,
                )
            )
        rows.append(jnp.concatenate(columns, axis=1))
    return jnp.concatenate(rows, axis=0)


def user_kernel(slots, count, users, items, values, out, places_out, buffer, places, arrivals):
    live = count[0]
    load_values(live, values, buffer, arrivals)
    buffer[MAXB] = jnp.full((EDGE, EDGE), -2.0, jnp.bfloat16)
    fill_places(live, slots, places)
    await_values(live, values, buffer, arrivals)

    def advance(pair, carry):
        rows = pl.ds(pl.multiple_of(pair * 2 * EDGE, 2 * EDGE), 2 * EDGE)
        user_pair = users[rows, :].astype(jnp.bfloat16)
        running = jnp.zeros((2 * EDGE, RANK), jnp.float32)
        for turn in range(IBLK // 2):
            item_pair = items[turn * 2 * EDGE : (turn + 1) * 2 * EDGE, :]
            error = square_error(
                user_pair, item_pair, pair * 2 * IBLK + turn * 2, places, buffer
            )
            running = running + dot_nn(error, item_pair)
        out[rows, :] = running.astype(jnp.bfloat16)
        return carry

    lax.fori_loop(0, UBLK // 2, advance, 0)
    for place in range(UBLK * IBLK):
        places_out[place] = places[place]


def item_kernel(count, places, users, items, values, out, buffer, turned, arrivals):
    live = count[0]
    load_values(live, values, buffer, arrivals)
    buffer[MAXB] = jnp.full((EDGE, EDGE), -2.0, jnp.bfloat16)
    for block in range(UBLK):
        turned[:, block * EDGE : (block + 1) * EDGE] = users[
            block * EDGE : (block + 1) * EDGE, :
        ].T
    await_values(live, values, buffer, arrivals)

    def advance(turn, carry):
        rows = pl.ds(pl.multiple_of(turn * 2 * EDGE, 2 * EDGE), 2 * EDGE)
        item_pair = items[rows, :]
        running = jnp.zeros((RANK, 2 * EDGE), jnp.float32)
        for pair in range(UBLK // 2):
            span = slice(pair * 2 * EDGE, (pair + 1) * 2 * EDGE)
            error = square_error(
                users[span, :], item_pair, pair * 2 * IBLK + turn * 2, places, buffer
            )
            running = running + dot_nn(turned[:, span], error)
        out[rows, :] = running.T.astype(jnp.bfloat16)
        return carry

    lax.fori_loop(0, IBLK // 2, advance, 0)


def whole(space):
    return pl.BlockSpec(memory_space=space)


def user_pass(slots, count, users, items, values):
    return pl.pallas_call(
        user_kernel,
        out_shape=(
            jax.ShapeDtypeStruct((UBLK * EDGE, RANK), jnp.bfloat16),
            jax.ShapeDtypeStruct((UBLK * IBLK,), jnp.int32),
        ),
        in_specs=[
            whole(pltpu.SMEM),
            whole(pltpu.SMEM),
            whole(pltpu.VMEM),
            whole(pltpu.VMEM),
            whole(pl.ANY),
        ],
        out_specs=(whole(pltpu.VMEM), whole(pltpu.SMEM)),
        scratch_shapes=[
            pltpu.VMEM((MAXB + 1, EDGE, EDGE), jnp.bfloat16),
            pltpu.SMEM((UBLK * IBLK,), jnp.int32),
            pltpu.SemaphoreType.DMA((MAXB // CHUNK,)),
        ],
        name="user_pass",
    )(slots, count, users, items, values)


def item_pass(count, places, users, items, values):
    return pl.pallas_call(
        item_kernel,
        out_shape=jax.ShapeDtypeStruct((IBLK * EDGE, RANK), jnp.bfloat16),
        in_specs=[
            whole(pltpu.SMEM),
            whole(pltpu.SMEM),
            whole(pltpu.VMEM),
            whole(pltpu.VMEM),
            whole(pl.ANY),
        ],
        out_specs=whole(pltpu.VMEM),
        scratch_shapes=[
            pltpu.VMEM((MAXB + 1, EDGE, EDGE), jnp.bfloat16),
            pltpu.VMEM((RANK, UBLK * EDGE), jnp.bfloat16),
            pltpu.SemaphoreType.DMA((MAXB // CHUNK,)),
        ],
        name="item_pass",
    )(count, places, users, items, values)


def on_device(
    user_factors,
    user_moment_one,
    user_moment_two,
    item_factors,
    item_moment_one,
    item_moment_two,
    block_slot,
    block_count,
    block_values,
):
    slots = block_slot.reshape(MAXB)
    count = block_count.reshape(1)
    values = block_values.reshape(MAXB, EDGE, EDGE)
    item_total = IBLK * EDGE * lax.axis_size(ITEMS)
    user_total = user_factors.shape[0] * lax.axis_size(USERS)
    items = lax.all_gather(item_factors.astype(jnp.bfloat16), USERS, axis=0, tiled=True)
    user_partial, places = user_pass(slots, count, user_factors, items, values)
    user_share = user_factors.shape[0] // lax.axis_size(ITEMS)
    user_offset = lax.axis_index(ITEMS) * user_share
    sent = user_partial.reshape(-1, user_share, RANK)
    got = lax.all_to_all(sent, ITEMS, 0, 0)
    user_sum = jnp.sum(got.astype(jnp.float32), axis=0)
    mine = functools.partial(
        lax.dynamic_slice_in_dim, start_index=user_offset, slice_size=user_share, axis=0
    )
    new_user, new_user_one, new_user_two = adam_update(
        mine(user_factors),
        mine(user_moment_one),
        mine(user_moment_two),
        user_sum,
        1.0 / math.sqrt(item_total),
    )
    new_low = lax.all_gather(new_user.astype(jnp.bfloat16), ITEMS, axis=0, tiled=True)
    item_partial = item_pass(count, places, new_low, items, values)
    item_share = item_factors.shape[0]
    sent = item_partial.reshape(-1, item_share, RANK)
    got = lax.all_to_all(sent, USERS, 0, 0)
    item_sum = jnp.sum(got.astype(jnp.float32), axis=0)
    new_item, new_item_one, new_item_two = adam_update(
        item_factors, item_moment_one, item_moment_two, item_sum, 1.0 / math.sqrt(user_total)
    )
    return (new_user, new_user_one, new_user_two, new_item, new_item_one, new_item_two)


def solution(mesh):
    fine = Mesh(mesh.devices.reshape(3, 8, 2, 4, 4), PARTS)
    return jax.shard_map(
        on_device,
        mesh=fine,
        in_specs=(
            P(USERS, None),
            P(USERS, None),
            P(USERS, None),
            P(ITEMS + USERS, None),
            P(ITEMS + USERS, None),
            P(ITEMS + USERS, None),
            P(USERS, ITEMS, None),
            P(USERS, ITEMS),
            P(USERS, ITEMS, None, None, None),
        ),
        out_specs=(
            P(USERS + ITEMS, None),
            P(USERS + ITEMS, None),
            P(USERS + ITEMS, None),
            P(ITEMS + USERS, None),
            P(ITEMS + USERS, None),
            P(ITEMS + USERS, None),
        ),
        check_vma=False,
    )
```

time: 934 us -> 207 us (0.22)
  waiting for transfers between devices: 759 us -> 15.7 us
  blocking collectives: 86.2 us -> 160 us
  other arithmetic: 29.4 us -> 3.12 us
  local copies, waits for them, and re-layouts: 25.8 us -> 0.02 us
  Pallas kernels: 0 us -> 19 us
  matrix products: 16.6 us -> 0 us
  between operations: 14.8 us -> 1.36 us
    psum x2 -> x0, waiting for transfers between devices: 759 us -> none  [the longest x1 563 us: on_device(): item_whole_sum = lax.psum(item_partial, 'users')]
    all_gather x1 -> x2, blocking collectives: 86.2 us -> 129 us  [the longest x1 90.1 us: on_device(): lax.all_gather(item_factors.astype(jnp.bfloat16), USERS, axis=0, tiled=True)]
    all_to_all x0 -> x1, blocking collectives: none -> 31.4 us  [on_device(): got = lax.all_to_all(sent, USERS, 0, 0)]
    pallas_call x0 -> x2, Pallas kernels: none -> 19 us  [the longest x1 9.94 us: user_pass(): pl.pallas_call(user_kernel, out_shape=(jax.ShapeDtypeStruct((UBLK * EDGE,...]
    dot_general x12 -> x0, matrix products: 16.6 us -> none  [the longest x6 8.29 us: advance(): jnp.einsum('kab,kbr->kar', weighted, item_rows, preferred_element_type=jn...]
    all_to_all x0 -> x1, waiting for transfers between devices: none -> 15.7 us  [on_device(): got = lax.all_to_all(sent, ITEMS, 0, 0)]
    gather x24 -> x0, local copies, waits for them, and re-layouts: 14.3 us -> none  [the longest x12 7.17 us: advance(): item_rows = item_panel[item_part]]
    scatter-add x12 -> x0, other arithmetic: 12.4 us -> none  [the longest x6 6.2 us: advance(): running.at[user_part]]
  transfers between devices with their start and end apart: 2 -> 1, of which waited for: 2 -> 1; matrix products, arithmetic and copies ran while one was open for 1% -> 0% of each run, Pallas kernels for 0% -> 0%
where the time goes in v1:
time: 207 us; the launch traced here: 206 us
  blocking collectives  160 us (77%)
  Pallas kernels  19 us (9%)
  waiting for transfers between devices  15.7 us (8%)
  starting transfers between devices  6.86 us (3%)
  other arithmetic  3.12 us (2%)
    all_gather x1, blocking collectives, on_device(): lax.all_gather(item_factors.astype(jnp.bfloat16), USERS, axis=0, tiled=True)  90.1 us
    all_gather x1, blocking collectives, on_device(): lax.all_gather(new_user.astype(jnp.bfloat16), ITEMS, axis=0, tiled=True)  38.7 us
    all_to_all x1, blocking collectives, on_device(): got = lax.all_to_all(sent, USERS, 0, 0)  31.4 us
    all_to_all x1, waiting for transfers between devices, on_device(): got = lax.all_to_all(sent, ITEMS, 0, 0)  15.7 us
    pallas_call x1, Pallas kernels, user_pass(): pl.pallas_call(user_kernel, out_shape=(jax.ShapeDtypeStruct((UBLK * EDGE,...  9.94 us
    pallas_call x1, Pallas kernels, item_pass(): pl.pallas_call(item_kernel, out_shape=jax.ShapeDtypeStruct((IBLK * EDGE,...  9.09 us
    all_to_all x1, starting transfers between devices, on_device(): got = lax.all_to_all(sent, ITEMS, 0, 0)  6.86 us
  transfers between devices with their start and end apart: 1, of which 1 were waited for; matrix products, arithmetic and copies ran while one was open for 0% of the time, Pallas kernels for 0%

profile of v1, /device:TPU:1, one launch (start us, length us, event | category | flops | bytes accessed | tf_op | source)
XLA Modules:
  0.0 206.3 jit_solution(14769206984214708886)
XLA Ops:
  1.3 0.7 convert_element_type.12
  2.0 90.1 %all_gather.6.items = bf16[1536,128]{1,0:T(8,128)(2,1)} all-gather(bf16[32,128]{1,0:T(8,128)(2,1)S(1)} %convert_element_type.12), channel_id=1, replica_groups=mesh['z_hi'=3,'y'=8,'core'=2,'x'=4,'z_lo'=4] {'z_hi','y','core'}, dimensions={0}, use_global_device_ids=true | all-gather | bytes 401408 | tf_op jit(solution)/shard_map/all_gather | solution.py:228
  92.1 9.9 %user_pass.1 = (bf16[2048,128]{1,0:T(8,128)(2,1)}, s32[192]{0:T(256)}) custom-call(s32[128]{0:T(128)} %bitcast.11, s32[1]{0:T(128)} %bitcast.5.count, f32[2048,128]{1,0:T(8,128)} %users.1, bf16[1536,128]{1,0:T(8,128)(2,1)} %all_gather.6.items, bf16[128,128,128]{2,1,0:T(8,128)(2,1)} %bitcast.7), custom_call_target="tpu_custom_call" | custom-call | tf_op jit(solution)/shard_map/user_pass/pallas_call | solution.py:168
  102.1 6.9 %all-to-all-start = ((bf16[16,128,128]{2,1,0:T(8,128)(2,1)}), bf16[16,128,128]{2,1,0:T(8,128)(2,1)S(1)}, u32[]{:S(2)}, u32[]{:S(2)}) async-start(bf16[16,128,128]{2,1,0:T(8,128)(2,1)} %bitcast.10), calls=%async_computation | async-start | bytes 1048576 | tf_op jit(solution)/shard_map/all_to_all | solution.py:233
  108.9 0.0 copy-start
  108.9 0.0 copy-start.1
  109.0 0.0 copy-start.2
  109.0 15.7 %all-to-all-done = bf16[16,128,128]{2,1,0:T(8,128)(2,1)S(1)} async-done(((bf16[16,128,128]{2,1,0:T(8,128)(2,1)}), bf16[16,128,128]{2,1,0:T(8,128)(2,1)S(1)}, u32[]{:S(2)}, u32[]{:S(2)}) %all-to-all-start) | async-done | bytes 524320 | tf_op jit(solution)/shard_map/all_to_all | solution.py:233
  124.7 0.1 convert_reduce_fusion
  124.8 1.6 fusion.3
  126.4 38.7 %all_gather.7.users = bf16[2048,128]{1,0:T(8,128)(2,1)} all-gather(bf16[128,128]{1,0:T(8,128)(2,1)S(1)} %get-tuple-element.13), channel_id=1, replica_groups=mesh['z_hi'=3,'y'=8,'core'=2,'x'=4,'z_lo'=4] {'x','z_lo'}, dimensions={0}, use_global_device_ids=true | all-gather | bytes 557056 | tf_op jit(solution)/shard_map/all_gather | solution.py:245
  165.1 9.1 %item_pass.1 = bf16[1536,128]{1,0:T(8,128)(2,1)} custom-call(s32[1]{0:T(128)} %bitcast.6.count, s32[192]{0:T(256)} %get-tuple-element.9.places, bf16[2048,128]{1,0:T(8,128)(2,1)} %all_gather.7.users, bf16[1536,128]{1,0:T(8,128)(2,1)} %all_gather.6.items, bf16[128,128,128]{2,1,0:T(8,128)(2,1)} %bitcast.8), custom_call_target="tpu_custom_call" | custom-call | tf_op jit(solution)/shard_map/item_pass/pallas_call | solution.py:192
  174.2 31.4 %all_to_all.10 = bf16[48,32,128]{2,1,0:T(8,128)(2,1)S(1)} all-to-all(bf16[48,32,128]{2,1,0:T(8,128)(2,1)} %bitcast.9), channel_id=1, replica_groups=mesh['z_hi'=3,'y'=8,'core'=2,'x'=4,'z_lo'=4] {'z_hi','y','core'}, dimensions={0} | all-to-all | bytes 786432 | tf_op jit(solution)/shard_map/all_to_all | solution.py:249
  205.6 0.1 convert_reduce_fusion.1
  205.6 0.0 copy-done
  205.6 0.0 copy-done.1
  205.7 0.0 copy-done.2
  205.7 0.6 multiply_subtract_fusion.1
Async XLA Ops:
  102.1 22.6 %all-to-all-start = ((bf16[16,128,128]{2,1,0:T(8,128)(2,1)}), bf16[16,128,128]{2,1,0:T(8,128)(2,1)S(1)}, u32[]{:S(2)}, u32[]{:S(2)}) async-start(bf16[16,128,128]{2,1,0:T(8,128)(2,1)} %bitcast.10), calls=%async_computation | async-start | bytes 1048576 | tf_op jit(solution)/shard_map/all_to_all | solution.py:233
  108.9 96.7 %copy-start = (f32[32,128]{1,0:T(8,128)S(1)}, f32[32,128]{1,0:T(8,128)}, u32[]{:S(2)}) copy-start(f32[32,128]{1,0:T(8,128)} %param.12) | copy-start | bytes 49156
  108.9 96.7 %copy-start.1 = (f32[32,128]{1,0:T(8,128)S(1)}, f32[32,128]{1,0:T(8,128)}, u32[]{:S(2)}) copy-start(f32[32,128]{1,0:T(8,128)} %param.13) | copy-start | bytes 49156
  109.0 96.7 %copy-start.2 = (f32[32,128]{1,0:T(8,128)S(1)}, f32[32,128]{1,0:T(8,128)}, u32[]{:S(2)}) copy-start(f32[32,128]{1,0:T(8,128)} %param.14) | copy-start | bytes 49156

commit v2 on v1

v2 whole, which is shorter than its diff:
```python
import functools
import math

import jax
import jax.numpy as jnp
from jax import lax
from jax.experimental import pallas as pl
from jax.experimental.pallas import tpu as pltpu
from jax.sharding import Mesh
from jax.sharding import PartitionSpec as P

conf_alpha = 0.5
reg_weight = 0.5
beta_one = 0.9
beta_two = 0.95
learn_rate = 0.1
adam_eps = 1e-08
correction_one = 1.0 - beta_one**11
correction_two = 1.0 - beta_two**11

EDGE = 128
RANK = 128
UBLK = 16
IBLK = 12
MAXB = 128
CHUNK = 8
PARTS = ("z_hi", "y", "core", "x", "z_lo")
USERS = PARTS[:3]
ITEMS = PARTS[3:]


def adam_update(parameter, first_moment, second_moment, grad_sum, grad_scale):
    gradient = grad_sum * grad_scale + reg_weight * parameter
    first_new = beta_one * first_moment + (1.0 - beta_one) * gradient
    second_new = beta_two * second_moment + (1.0 - beta_two) * gradient * gradient
    step_size = first_new / correction_one / (jnp.sqrt(second_new / correction_two) + adam_eps)
    return (parameter - learn_rate * step_size, first_new, second_new)


def dot_nt(left, right):
    return lax.dot_general(
        left, right, (((1,), (1,)), ((), ())), preferred_element_type=jnp.float32
    )


def dot_nn(left, right):
    return lax.dot_general(
        left, right, (((1,), (0,)), ((), ())), preferred_element_type=jnp.float32
    )


def fill_places(count, slots, places):
    for place in range(UBLK * IBLK):
        places[place] = MAXB

    def advance(turn, carry):
        for inner in range(CHUNK):
            listed = turn * CHUNK + inner
            place = slots[listed]
            places[place] = jnp.where(listed < count, listed, places[place])
        return carry

    lax.fori_loop(0, (count + CHUNK - 1) // CHUNK, advance, 0)


def value_copies(values, buffer, arrivals):
    return [
        pltpu.make_async_copy(
            values.at[pl.ds(chunk * CHUNK, CHUNK)],
            buffer.at[pl.ds(chunk * CHUNK, CHUNK)],
            arrivals.at[chunk],
        )
        for chunk in range(MAXB // CHUNK)
    ]


def weighted(predicted, place, values):
    live = place < MAXB
    base = jnp.where(live, 1.0, 0.0).astype(jnp.float32)
    slope = jnp.where(live, conf_alpha, 0.0).astype(jnp.float32)
    target = values[jnp.minimum(place, MAXB - 1)].astype(jnp.float32)
    return ((base + slope * target) * (predicted - target)).astype(jnp.bfloat16)


def square_error(user_pair, item_pair, first_place, places, values):
    predicted = dot_nt(user_pair, item_pair)
    rows = []
    for row in range(2):
        columns = []
        for column in range(2):
            part = predicted[row * EDGE : (row + 1) * EDGE, column * EDGE : (column + 1) * EDGE]
            columns.append(weighted(part, places[first_place + row * IBLK + column], values))
        rows.append(jnp.concatenate(columns, axis=1))
    return jnp.concatenate(rows, axis=0)


def user_kernel(
    slots, count, users, gathered, values, out, panel, places_out, places, low, buffer, arrivals, ready
):
    copies = value_copies(values, buffer, arrivals)
    fetch = pltpu.make_async_copy(users, low, ready)
    fetch.start()
    for copy in copies:
        copy.start()
    fill_places(count[0], slots, places)
    share = gathered.shape[2]
    for rank in range(gathered.shape[1]):
        for core in range(2):
            first = (rank * 2 + core) * share
            panel[first : first + share, :] = gathered[core, rank]
    for place in range(UBLK * IBLK):
        places_out[place] = places[place]
    fetch.wait()
    for copy in copies:
        copy.wait()

    def advance(pair, carry):
        rows = pl.ds(pl.multiple_of(pair * 2 * EDGE, 2 * EDGE), 2 * EDGE)
        user_pair = low[rows, :].astype(jnp.bfloat16)
        running = jnp.zeros((2 * EDGE, RANK), jnp.float32)
        for turn in range(IBLK // 2):
            item_pair = panel[turn * 2 * EDGE : (turn + 1) * 2 * EDGE, :]
            error = square_error(
                user_pair, item_pair, pair * 2 * IBLK + turn * 2, places, buffer
            )
            running = running + dot_nn(error, item_pair)
        out[rows, :] = running.astype(jnp.bfloat16)
        return carry

    lax.fori_loop(0, UBLK // 2, advance, 0)


def item_kernel(core, places, users, items, values, keep, sent, turned, buffer, arrivals):
    copies = value_copies(values, buffer, arrivals)
    for copy in copies:
        copy.start()
    for block in range(UBLK):
        turned[:, block * EDGE : (block + 1) * EDGE] = users[
            block * EDGE : (block + 1) * EDGE, :
        ].T
    share = keep.shape[1]
    ranks = EDGE // share
    first_core = core[0] == 0
    for copy in copies:
        copy.wait()

    def advance(turn, carry):
        rows = pl.ds(pl.multiple_of(turn * 2 * EDGE, 2 * EDGE), 2 * EDGE)
        item_pair = items[rows, :]
        running = jnp.zeros((RANK, 2 * EDGE), jnp.float32)
        for pair in range(UBLK // 2):
            span = slice(pair * 2 * EDGE, (pair + 1) * 2 * EDGE)
            error = square_error(
                users[span, :], item_pair, pair * 2 * IBLK + turn * 2, places, buffer
            )
            running = running + dot_nn(turned[:, span], error)
        split = running.T.reshape(ranks, 2, share, RANK)
        even, odd = split[:, 0], split[:, 1]
        where = pl.ds(turn * ranks, ranks)
        keep[where] = jnp.where(first_core, even, odd)
        sent[where] = jnp.where(first_core, odd, even).astype(jnp.bfloat16)
        return carry

    lax.fori_loop(0, IBLK // 2, advance, 0)


def whole(space):
    return pl.BlockSpec(memory_space=space)


def user_pass(slots, count, users, gathered, values):
    panel = (gathered.shape[0] * gathered.shape[1] * gathered.shape[2], RANK)
    return pl.pallas_call(
        user_kernel,
        out_shape=(
            jax.ShapeDtypeStruct((UBLK * EDGE, RANK), jnp.bfloat16),
            jax.ShapeDtypeStruct(panel, jnp.bfloat16),
            jax.ShapeDtypeStruct((UBLK * IBLK,), jnp.int32),
        ),
        in_specs=[
            whole(pltpu.SMEM),
            whole(pltpu.SMEM),
            whole(pltpu.HBM),
            whole(pltpu.VMEM),
            whole(pltpu.HBM),
        ],
        out_specs=(whole(pltpu.VMEM), whole(pltpu.VMEM), whole(pltpu.SMEM)),
        scratch_shapes=[
            pltpu.SMEM((UBLK * IBLK,), jnp.int32),
            pltpu.VMEM((UBLK * EDGE, RANK), jnp.float32),
            pltpu.VMEM((MAXB, EDGE, EDGE), jnp.bfloat16),
            pltpu.SemaphoreType.DMA((MAXB // CHUNK,)),
            pltpu.SemaphoreType.DMA,
        ],
        name="user_pass",
    )(slots, count, users, gathered, values)


def item_pass(core, places, users, items, values, share):
    ranks = items.shape[0] // (2 * share)
    return pl.pallas_call(
        item_kernel,
        out_shape=(
            jax.ShapeDtypeStruct((ranks, share, RANK), jnp.float32),
            jax.ShapeDtypeStruct((ranks, share, RANK), jnp.bfloat16),
        ),
        in_specs=[
            whole(pltpu.SMEM),
            whole(pltpu.SMEM),
            whole(pltpu.VMEM),
            whole(pltpu.VMEM),
            whole(pltpu.HBM),
        ],
        out_specs=(whole(pltpu.VMEM), whole(pltpu.VMEM)),
        scratch_shapes=[
            pltpu.VMEM((RANK, UBLK * EDGE), jnp.bfloat16),
            pltpu.VMEM((MAXB, EDGE, EDGE), jnp.bfloat16),
            pltpu.SemaphoreType.DMA((MAXB // CHUNK,)),
        ],
        name="item_pass",
    )(core, places, users, items, values)


def spread(mine, axes):
    ranks = lax.axis_size(axes)
    return lax.all_to_all(jnp.broadcast_to(mine[None], (ranks,) + mine.shape), axes, 0, 0)


def on_device(
    user_factors,
    user_moment_one,
    user_moment_two,
    item_factors,
    item_moment_one,
    item_moment_two,
    block_slot,
    block_count,
    block_values,
):
    slots = block_slot.reshape(MAXB)
    count = block_count.reshape(1)
    values = block_values.reshape(MAXB, EDGE, EDGE)
    item_total = IBLK * EDGE * lax.axis_size(ITEMS)
    user_total = user_factors.shape[0] * lax.axis_size(USERS)
    half = spread(item_factors.astype(jnp.bfloat16), ("z_hi", "y"))
    gathered = lax.all_gather(half, "core", axis=0)
    user_partial, items, places = user_pass(slots, count, user_factors, gathered, values)
    user_share = user_factors.shape[0] // lax.axis_size(ITEMS)
    user_offset = lax.axis_index(ITEMS) * user_share
    sent = user_partial.reshape(-1, user_share, RANK)
    got = lax.all_to_all(sent, ITEMS, 0, 0)
    user_sum = jnp.sum(got.astype(jnp.float32), axis=0)
    mine = functools.partial(
        lax.dynamic_slice_in_dim, start_index=user_offset, slice_size=user_share, axis=0
    )
    new_user, new_user_one, new_user_two = adam_update(
        mine(user_factors),
        mine(user_moment_one),
        mine(user_moment_two),
        user_sum,
        1.0 / math.sqrt(item_total),
    )
    new_low = spread(new_user.astype(jnp.bfloat16), ITEMS).reshape(-1, RANK)
    core = lax.axis_index("core").reshape(1)
    keep, sent = item_pass(core, places, new_low, items, values, item_factors.shape[0])
    other = lax.ppermute(sent, "core", [(0, 1), (1, 0)])
    both = (keep + other.astype(jnp.float32)).astype(jnp.bfloat16)
    got = lax.all_to_all(both, ("z_hi", "y"), 0, 0)
    item_sum = jnp.sum(got.astype(jnp.float32), axis=0)
    new_item, new_item_one, new_item_two = adam_update(
        item_factors, item_moment_one, item_moment_two, item_sum, 1.0 / math.sqrt(user_total)
    )
    return (new_user, new_user_one, new_user_two, new_item, new_item_one, new_item_two)


def solution(mesh):
    fine = Mesh(mesh.devices.reshape(3, 8, 2, 4, 4), PARTS)
    return jax.shard_map(
        on_device,
        mesh=fine,
        in_specs=(
            P(USERS, None),
            P(USERS, None),
            P(USERS, None),
            P(ITEMS + USERS, None),
            P(ITEMS + USERS, None),
            P(ITEMS + USERS, None),
            P(USERS, ITEMS, None),
            P(USERS, ITEMS),
            P(USERS, ITEMS, None, None, None),
        ),
        out_specs=(
            P(USERS + ITEMS, None),
            P(USERS + ITEMS, None),
            P(USERS + ITEMS, None),
            P(ITEMS + USERS, None),
            P(ITEMS + USERS, None),
            P(ITEMS + USERS, None),
        ),
        check_vma=False,
    )
```

time: 207 us -> 134 us (0.65)
  blocking collectives: 160 us -> 23.7 us
  starting transfers between devices: 6.86 us -> 37.4 us
  waiting for transfers between devices: 15.7 us -> 44.1 us
  local copies, waits for them, and re-layouts: 0.02 us -> 2.42 us
    all_gather x2 -> x1, blocking collectives: 129 us -> 4.07 us  [on_device(): gathered = lax.all_gather(half, 'core', axis=0)]
    all_to_all x0 -> x2, waiting for transfers between devices: none -> 27.1 us  [spread(): lax.all_to_all(jnp.broadcast_to(mine[None], (ranks,) + mine.shape), axes,...]
    all_to_all x0 -> x2, starting transfers between devices: none -> 24.1 us  [spread(): lax.all_to_all(jnp.broadcast_to(mine[None], (ranks,) + mine.shape), axes,...]
    all_to_all x1, blocking collectives: 31.4 us -> 19.7 us  [on_device(): got = lax.all_to_all(both, ('z_hi', 'y'), 0, 0)]
    ppermute x0 -> x1, starting transfers between devices: none -> 3.58 us  [on_device(): other = lax.ppermute(sent, 'core', [(0, 1), (1, 0)])]
    all_to_all x1, starting transfers between devices: 6.86 us -> 9.78 us  [on_device(): got = lax.all_to_all(sent, ITEMS, 0, 0)]
  transfers between devices with their start and end apart: 1 -> 4, of which waited for: 1 -> 4; matrix products, arithmetic and copies ran while one was open for 0% -> 0% of each run, Pallas kernels for 0% -> 0%
where the time goes in v2:
time: 134 us
  waiting for transfers between devices  44.1 us (33%)
  starting transfers between devices  37.4 us (28%)
  blocking collectives  23.7 us (18%)
  Pallas kernels  20.4 us (15%)
  other arithmetic  4.14 us (3%)
  local copies, waits for them, and re-layouts  2.42 us (2%)
  between operations  1.39 us (1%)
    all_to_all x2, waiting for transfers between devices, spread(): lax.all_to_all(jnp.broadcast_to(mine[None], (ranks,) + mine.shape), axes,...  27.1 us
    all_to_all x2, starting transfers between devices, spread(): lax.all_to_all(jnp.broadcast_to(mine[None], (ranks,) + mine.shape), axes,...  24.1 us
    all_to_all x1, blocking collectives, on_device(): got = lax.all_to_all(both, ('z_hi', 'y'), 0, 0)  19.7 us
    all_to_all x1, waiting for transfers between devices, on_device(): got = lax.all_to_all(sent, ITEMS, 0, 0)  15.8 us
    pallas_call x1, Pallas kernels, user_pass(): pl.pallas_call(user_kernel, out_shape=(jax.ShapeDtypeStruct((UBLK * EDGE,...  10.6 us
    pallas_call x1, Pallas kernels, item_pass(): pl.pallas_call(item_kernel, out_shape=(jax.ShapeDtypeStruct((ranks, share...  9.81 us
    all_to_all x1, starting transfers between devices, on_device(): got = lax.all_to_all(sent, ITEMS, 0, 0)  9.78 us
    all_gather x1, blocking collectives, on_device(): gathered = lax.all_gather(half, 'core', axis=0)  4.07 us
  transfers between devices with their start and end apart: 4, of which 4 were waited for; matrix products, arithmetic and copies ran while one was open for 0% of the time, Pallas kernels for 0%

profile of v2, /device:TPU:1, one launch (start us, length us, event | category | flops | bytes accessed | tf_op | source)
XLA Modules:
  0.0 133.6 jit_solution(4677065578945281558)
XLA Ops:
  0.6 0.7 convert_element_type.18
  1.4 0.7 broadcast_in_dim.4
  2.1 20.0 %all-to-all-start = ((bf16[24,32,128]{2,1,0:T(8,128)(2,1)}), bf16[24,32,128]{2,1,0:T(8,128)(2,1)S(1)}, u32[]{:S(2)}, u32[]{:S(2)}) async-start(bf16[24,32,128]{2,1,0:T(8,128)(2,1)} %broadcast_in_dim.4), calls=%async_computation | async-start | bytes 393216 | tf_op jit(solution)/shard_map/all_to_all | solution.py:226
  22.7 11.3 %all-to-all-done = bf16[24,32,128]{2,1,0:T(8,128)(2,1)S(1)} async-done(((bf16[24,32,128]{2,1,0:T(8,128)(2,1)}), bf16[24,32,128]{2,1,0:T(8,128)(2,1)S(1)}, u32[]{:S(2)}, u32[]{:S(2)}) %all-to-all-start) | async-done | bytes 196640 | tf_op jit(solution)/shard_map/all_to_all | solution.py:226
  34.0 4.1 %all-gather = bf16[48,32,128]{2,1,0:T(8,128)(2,1)} all-gather(bf16[24,32,128]{2,1,0:T(8,128)(2,1)S(1)} %all-to-all-done), channel_id=2, replica_groups=mesh['z_hi'=3,'y'=8,'core'=2,'x'=4,'z_lo'=4] {'core'}, dimensions={0}, use_global_device_ids=true | all-gather | bytes 589824 | tf_op jit(solution)/shard_map/all_gather | solution.py:246
  38.1 10.6 %user_pass.1 = (bf16[2048,128]{1,0:T(8,128)(2,1)}, bf16[1536,128]{1,0:T(8,128)(2,1)}, s32[192]{0:T(256)}) custom-call(s32[128]{0:T(128)} %bitcast.13, s32[1]{0:T(128)} %bitcast.7.count, f32[2048,128]{1,0:T(8,128)} %users.1, bf16[2,24,32,128]{3,2,1,0:T(8,128)(2,1)} %bitcast.11, bf16[128,128,128]{2,1,0:T(8,128)(2,1)} %bitcast.8), custom_call_target="tpu_custom_call" | custom-call | tf_op jit(solution)/shard_map/user_pass/pallas_call | solution.py:173
  48.6 9.8 %all-to-all-start.1 = ((bf16[16,128,128]{2,1,0:T(8,128)(2,1)}), bf16[16,128,128]{2,1,0:T(8,128)(2,1)S(1)}, u32[]{:S(2)}, u32[]{:S(2)}) async-start(bf16[16,128,128]{2,1,0:T(8,128)(2,1)} %bitcast.12), calls=%async_computation.1 | async-start | bytes 1048576 | tf_op jit(solution)/shard_map/all_to_all | solution.py:251
  58.4 15.8 %all-to-all-done.1 = bf16[16,128,128]{2,1,0:T(8,128)(2,1)S(1)} async-done(((bf16[16,128,128]{2,1,0:T(8,128)(2,1)}), bf16[16,128,128]{2,1,0:T(8,128)(2,1)S(1)}, u32[]{:S(2)}, u32[]{:S(2)}) %all-to-all-start.1) | async-done | bytes 524320 | tf_op jit(solution)/shard_map/all_to_all | solution.py:251
  74.2 0.1 convert_reduce_fusion
  74.3 0.0 copy-start.1
  74.3 0.0 copy-start.2
  74.3 0.0 copy-start.3
  74.3 1.6 %fusion.3 = (bf16[128,128]{1,0:T(8,128)(2,1)S(1)}, f32[128,128]{1,0:T(8,128)}, f32[128,128]{1,0:T(8,128)}, f32[128,128]{1,0:T(8,128)}) fusion(f32[2048,128]{1,0:T(8,128)} %users.1, s32[]{:T(128)S(6)} %select_n.2, f32[128,128]{1,0:T(8,128)S(1)} %convert_reduce_fusion, f32[2048,128]{1,0:T(8,128)} %param.10, f32[2048,128]{1,0:T(8,128)} %param.11), kind=kLoop, calls=%fused_computation.13 | loop fusion | flops 278528 | bytes 491524 | tf_op jit(solution)/shard_map/convert_element_type | solution.py:263
  75.9 0.9 broadcast_in_dim.5
  76.8 4.1 %all-to-all-start.2 = ((bf16[16,128,128]{2,1,0:T(8,128)(2,1)}), bf16[16,128,128]{2,1,0:T(8,128)(2,1)S(1)}, u32[]{:S(2)}, u32[]{:S(2)}) async-start(bf16[16,128,128]{2,1,0:T(8,128)(2,1)} %broadcast_in_dim.5), calls=%async_computation.2 | async-start | bytes 1048576 | tf_op jit(solution)/shard_map/all_to_all | solution.py:226
  80.9 15.8 %all-to-all-done.2 = bf16[16,128,128]{2,1,0:T(8,128)(2,1)S(1)} async-done(((bf16[16,128,128]{2,1,0:T(8,128)(2,1)}), bf16[16,128,128]{2,1,0:T(8,128)(2,1)S(1)}, u32[]{:S(2)}, u32[]{:S(2)}) %all-to-all-start.2) | async-done | bytes 524320 | tf_op jit(solution)/shard_map/all_to_all | solution.py:226
  96.7 0.8 copy-done
  97.5 9.8 %item_pass.1 = (f32[24,32,128]{2,1,0:T(8,128)}, bf16[24,32,128]{2,1,0:T(8,128)(2,1)}) custom-call(s32[1]{0:T(128)} %bitcast.5.core, s32[192]{0:T(256)} %get-tuple-element.12.places, bf16[2048,128]{1,0:T(8,128)(2,1)} %bitcast.10, bf16[1536,128]{1,0:T(8,128)(2,1)} %get-tuple-element.13.items, bf16[128,128,128]{2,1,0:T(8,128)(2,1)} %bitcast.9), custom_call_target="tpu_custom_call" | custom-call | tf_op jit(solution)/shard_map/item_pass/pallas_call | solution.py:201
  107.3 3.6 %collective-permute-start = (bf16[24,32,128]{2,1,0:T(8,128)(2,1)}, bf16[24,32,128]{2,1,0:T(8,128)(2,1)S(1)}, u32[]{:S(2)}, u32[]{:S(2)}) collective-permute-start(bf16[24,32,128]{2,1,0:T(8,128)(2,1)} %get-tuple-element.15), channel_id=1, source_target_pairs={{0,16},{16,0},{1,17},{17,1},{2,18},{18,2},{3,19},{19,3},{4,20},{20... | collective-permute-start | bytes 589832 | tf_op jit(solution)/shard_map/ppermute | solution.py:266
  110.9 1.3 collective-permute-done
  112.2 1.0 add_convert_fusion
  113.2 19.7 %all_to_all.20 = bf16[24,32,128]{2,1,0:T(8,128)(2,1)S(1)} all-to-all(bf16[24,32,128]{2,1,0:T(8,128)(2,1)S(1)} %add_convert_fusion), channel_id=1, replica_groups=mesh['z_hi'=3,'y'=8,'core'=2,'x'=4,'z_lo'=4] {'z_hi','y'}, dimensions={0} | all-to-all | bytes 393216 | tf_op jit(solution)/shard_map/all_to_all | solution.py:268
  132.9 0.0 copy-done.2
  132.9 0.6 multiply_subtract_fusion.1
  (4 shorter events, 0.0 us)
Async XLA Ops:
  2.1 31.9 %all-to-all-start = ((bf16[24,32,128]{2,1,0:T(8,128)(2,1)}), bf16[24,32,128]{2,1,0:T(8,128)(2,1)S(1)}, u32[]{:S(2)}, u32[]{:S(2)}) async-start(bf16[24,32,128]{2,1,0:T(8,128)(2,1)} %broadcast_in_dim.4), calls=%async_computation | async-start | bytes 393216 | tf_op jit(solution)/shard_map/all_to_all | solution.py:226
  48.6 25.6 %all-to-all-start.1 = ((bf16[16,128,128]{2,1,0:T(8,128)(2,1)}), bf16[16,128,128]{2,1,0:T(8,128)(2,1)S(1)}, u32[]{:S(2)}, u32[]{:S(2)}) async-start(bf16[16,128,128]{2,1,0:T(8,128)(2,1)} %bitcast.12), calls=%async_computation.1 | async-start | bytes 1048576 | tf_op jit(solution)/shard_map/all_to_all | solution.py:251
  74.3 58.6 %copy-start.1 = (f32[32,128]{1,0:T(8,128)S(1)}, f32[32,128]{1,0:T(8,128)}, u32[]{:S(2)}) copy-start(f32[32,128]{1,0:T(8,128)} %param.12) | copy-start | bytes 49156
  74.3 58.6 %copy-start.2 = (f32[32,128]{1,0:T(8,128)S(1)}, f32[32,128]{1,0:T(8,128)}, u32[]{:S(2)}) copy-start(f32[32,128]{1,0:T(8,128)} %param.13) | copy-start | bytes 49156
  74.3 58.6 %copy-start.3 = (f32[32,128]{1,0:T(8,128)S(1)}, f32[32,128]{1,0:T(8,128)}, u32[]{:S(2)}) copy-start(f32[32,128]{1,0:T(8,128)} %param.14) | copy-start | bytes 49156
  76.8 19.9 %all-to-all-start.2 = ((bf16[16,128,128]{2,1,0:T(8,128)(2,1)}), bf16[16,128,128]{2,1,0:T(8,128)(2,1)S(1)}, u32[]{:S(2)}, u32[]{:S(2)}) async-start(bf16[16,128,128]{2,1,0:T(8,128)(2,1)} %broadcast_in_dim.5), calls=%async_computation.2 | async-start | bytes 1048576 | tf_op jit(solution)/shard_map/all_to_all | solution.py:226
  96.7 0.8 copy-start
  107.3 4.9 %collective-permute-start = (bf16[24,32,128]{2,1,0:T(8,128)(2,1)}, bf16[24,32,128]{2,1,0:T(8,128)(2,1)S(1)}, u32[]{:S(2)}, u32[]{:S(2)}) collective-permute-start(bf16[24,32,128]{2,1,0:T(8,128)(2,1)} %get-tuple-element.15), channel_id=1, source_target_pairs={{0,16},{16,0},{1,17},{17,1},{2,18},{18,2},{3,19},{19,3},{4,20},{20... | collective-permute-start | bytes 589832 | tf_op jit(solution)/shard_map/ppermute | solution.py:266

commit v3 on v2

--- a/solution.py
+++ b/solution.py
@@ -117,17 +117,17 @@
     def advance(pair, carry):
         rows = pl.ds(pl.multiple_of(pair * 2 * EDGE, 2 * EDGE), 2 * EDGE)
         user_pair = low[rows, :].astype(jnp.bfloat16)
-        running = jnp.zeros((2 * EDGE, RANK), jnp.float32)
+        errors = []
         for turn in range(IBLK // 2):
             item_pair = panel[turn * 2 * EDGE : (turn + 1) * 2 * EDGE, :]
-            error = square_error(
-                user_pair, item_pair, pair * 2 * IBLK + turn * 2, places, buffer
+            errors.append(
+                square_error(user_pair, item_pair, pair * 2 * IBLK + turn * 2, places, buffer)
             )
-            running = running + dot_nn(error, item_pair)
-        out[rows, :] = running.astype(jnp.bfloat16)
+        total = dot_nn(jnp.concatenate(errors, axis=1), panel[...])
+        out[rows, :] = total.astype(jnp.bfloat16)
         return carry
 
-    lax.fori_loop(0, UBLK // 2, advance, 0)
+    lax.fori_loop(0, UBLK // 2, advance, 0, unroll=4)
 
 
 def item_kernel(core, places, users, items, values, keep, sent, turned, buffer, arrivals):
@@ -147,13 +147,13 @@
     def advance(turn, carry):
         rows = pl.ds(pl.multiple_of(turn * 2 * EDGE, 2 * EDGE), 2 * EDGE)
         item_pair = items[rows, :]
-        running = jnp.zeros((RANK, 2 * EDGE), jnp.float32)
+        errors = []
         for pair in range(UBLK // 2):
             span = slice(pair * 2 * EDGE, (pair + 1) * 2 * EDGE)
-            error = square_error(
-                users[span, :], item_pair, pair * 2 * IBLK + turn * 2, places, buffer
+            errors.append(
+                square_error(users[span, :], item_pair, pair * 2 * IBLK + turn * 2, places, buffer)
             )
-            running = running + dot_nn(turned[:, span], error)
+        running = dot_nn(turned[...], jnp.concatenate(errors, axis=0))
         split = running.T.reshape(ranks, 2, share, RANK)
         even, odd = split[:, 0], split[:, 1]
         where = pl.ds(turn * ranks, ranks)
@@ -161,11 +161,53 @@
         sent[where] = jnp.where(first_core, odd, even).astype(jnp.bfloat16)
         return carry
 
-    lax.fori_loop(0, IBLK // 2, advance, 0)
+    lax.fori_loop(0, IBLK // 2, advance, 0, unroll=3)
+
+
+def user_update_kernel(
+    offset, got, parameter, first, second, new, new_first, new_second, shared, mine, arrivals, scale
+):
+    rows = pl.ds(pl.multiple_of(offset[0], EDGE), EDGE)
+    copies = [
+        pltpu.make_async_copy(source.at[rows], mine.at[place], arrivals.at[place])
+        for place, source in enumerate((parameter, first, second))
+    ]
+    for copy in copies:
+        copy.start()
+    total = got[0].astype(jnp.float32)
+    for rank in range(1, got.shape[0]):
+        total = total + got[rank].astype(jnp.float32)
+    for copy in copies:
+        copy.wait()
+    updated = adam_update(mine[0], mine[1], mine[2], total, scale)
+    new[...], new_first[...], new_second[...] = updated
+    low = updated[0].astype(jnp.bfloat16)
+    for rank in range(got.shape[0]):
+        shared[rank] = low
+
+
+def share_kernel(items, shared):
+    low = items[...].astype(jnp.bfloat16)
+    for rank in range(shared.shape[0]):
+        shared[rank] = low
 
 
 def whole(space):
     return pl.BlockSpec(memory_space=space)
+
+
+def grant(mebibytes):
+    return pltpu.CompilerParams(vmem_limit_bytes=mebibytes * 1024 * 1024)
+
+
+def share_items(items, ranks):
+    return pl.pallas_call(
+        share_kernel,
+        out_shape=jax.ShapeDtypeStruct((ranks,) + items.shape, jnp.bfloat16),
+        in_specs=[whole(pltpu.VMEM)],
+        out_specs=whole(pltpu.VMEM),
+        name="share_items",
+    )(items)
 
 
 def user_pass(slots, count, users, gathered, values):
@@ -192,6 +234,7 @@
             pltpu.SemaphoreType.DMA((MAXB // CHUNK,)),
             pltpu.SemaphoreType.DMA,
         ],
+        compiler_params=grant(16),
         name="user_pass",
     )(slots, count, users, gathered, values)
 
@@ -217,13 +260,29 @@
             pltpu.VMEM((MAXB, EDGE, EDGE), jnp.bfloat16),
             pltpu.SemaphoreType.DMA((MAXB // CHUNK,)),
         ],
+        compiler_params=grant(16),
         name="item_pass",
     )(core, places, users, items, values)
 
 
-def spread(mine, axes):
-    ranks = lax.axis_size(axes)
-    return lax.all_to_all(jnp.broadcast_to(mine[None], (ranks,) + mine.shape), axes, 0, 0)
+def user_update(offset, got, parameter, first, second, scale):
+    share = jax.ShapeDtypeStruct((EDGE, RANK), jnp.float32)
+    return pl.pallas_call(
+        functools.partial(user_update_kernel, scale=scale),
+        out_shape=(share, share, share, jax.ShapeDtypeStruct(got.shape, jnp.bfloat16)),
+        in_specs=[whole(pltpu.SMEM), whole(pltpu.VMEM)] + [whole(pltpu.HBM)] * 3,
+        out_specs=(whole(pltpu.VMEM),) * 4,
+        scratch_shapes=[
+            pltpu.VMEM((3, EDGE, RANK), jnp.float32),
+            pltpu.SemaphoreType.DMA((3,)),
+        ],
+        compiler_params=grant(16),
+        name="user_update",
+    )(offset, got, parameter, first, second)
+
+
+def far(array):
+    return pltpu.with_memory_space_constraint(array, pltpu.HBM)
 
 
 def on_device(
@@ -239,28 +298,22 @@
 ):
     slots = block_slot.reshape(MAXB)
     count = block_count.reshape(1)
-    values = block_values.reshape(MAXB, EDGE, EDGE)
+    values = far(block_values.reshape(MAXB, EDGE, EDGE))
+    user_state = [far(array) for array in (user_factors, user_moment_one, user_moment_two)]
     item_total = IBLK * EDGE * lax.axis_size(ITEMS)
     user_total = user_factors.shape[0] * lax.axis_size(USERS)
-    half = spread(item_factors.astype(jnp.bfloat16), ("z_hi", "y"))
+    shared = share_items(item_factors, lax.axis_size(("z_hi", "y")))
+    half = lax.all_to_all(shared, ("z_hi", "y"), 0, 0)
     gathered = lax.all_gather(half, "core", axis=0)
-    user_partial, items, places = user_pass(slots, count, user_factors, gathered, values)
+    user_partial, items, places = user_pass(slots, count, user_state[0], gathered, values)
     user_share = user_factors.shape[0] // lax.axis_size(ITEMS)
     user_offset = lax.axis_index(ITEMS) * user_share
     sent = user_partial.reshape(-1, user_share, RANK)
     got = lax.all_to_all(sent, ITEMS, 0, 0)
-    user_sum = jnp.sum(got.astype(jnp.float32), axis=0)
-    mine = functools.partial(
-        lax.dynamic_slice_in_dim, start_index=user_offset, slice_size=user_share, axis=0
-    )
-    new_user, new_user_one, new_user_two = adam_update(
-        mine(user_factors),
-        mine(user_moment_one),
-        mine(user_moment_two),
-        user_sum,
-        1.0 / math.sqrt(item_total),
-    )
-    new_low = spread(new_user.astype(jnp.bfloat16), ITEMS).reshape(-1, RANK)
+    new_user, new_user_one, new_user_two, shared = user_update(
+        user_offset.reshape(1), got, *user_state, 1.0 / math.sqrt(item_total)
+    )
+    new_low = lax.all_to_all(shared, ITEMS, 0, 0).reshape(-1, RANK)
     core = lax.axis_index("core").reshape(1)
     keep, sent = item_pass(core, places, new_low, items, values, item_factors.shape[0])
     other = lax.ppermute(sent, "core", [(0, 1), (1, 0)])

time: 134 us -> 127 us (0.948)
  other arithmetic: 4.14 us -> 0.72 us
  Pallas kernels: 20.4 us -> 18.3 us
  local copies, waits for them, and re-layouts: 2.42 us -> 0.67 us
    pallas_call x0 -> x2, Pallas kernels: none -> 3.27 us  [the longest x1 1.86 us: user_update(): pl.pallas_call(functools.partial(user_update_kernel, scale=scale), out_sh...]
    pallas_call x1, Pallas kernels: 9.81 us -> 6.68 us  [item_pass(): pl.pallas_call(item_kernel, out_shape=(jax.ShapeDtypeStruct((ranks, share...]
    convert_element_type x2 -> x0, other arithmetic: 2.34 us -> none  [the longest x1 1.62 us: on_device(): new_low = spread(new_user.astype(jnp.bfloat16), ITEMS).reshape(-1, RANK)]
    pallas_call x1, Pallas kernels: 10.6 us -> 8.36 us  [user_pass(): pl.pallas_call(user_kernel, out_shape=(jax.ShapeDtypeStruct((UBLK * EDGE,...]
    broadcast_in_dim x2 -> x0, local copies, waits for them, and re-layouts: 1.6 us -> none  [spread(): jnp.broadcast_to(mine[None], (ranks,) + mine.shape)]
where the time goes in v3:
time: 127 us; the launch traced here: 126 us
  waiting for transfers between devices  43.9 us (35%)
  starting transfers between devices  37.6 us (30%)
  blocking collectives  23.6 us (19%)
  Pallas kernels  18.3 us (14%)
  between operations  1.4 us (1%)
    all_to_all x1, starting transfers between devices, on_device(): half = lax.all_to_all(shared, ('z_hi', 'y'), 0, 0)  20 us
    all_to_all x1, blocking collectives, on_device(): got = lax.all_to_all(both, ('z_hi', 'y'), 0, 0)  19.6 us
    all_to_all x1, waiting for transfers between devices, on_device(): new_low = lax.all_to_all(shared, ITEMS, 0, 0).reshape(-1, RANK)  15.8 us
    all_to_all x1, waiting for transfers between devices, on_device(): got = lax.all_to_all(sent, ITEMS, 0, 0)  15.8 us
    all_to_all x1, waiting for transfers between devices, on_device(): half = lax.all_to_all(shared, ('z_hi', 'y'), 0, 0)  11.3 us
    all_to_all x1, starting transfers between devices, on_device(): got = lax.all_to_all(sent, ITEMS, 0, 0)  9.79 us
    pallas_call x1, Pallas kernels, user_pass(): pl.pallas_call(user_kernel, out_shape=(jax.ShapeDtypeStruct((UBLK * EDGE,...  8.36 us
    pallas_call x1, Pallas kernels, item_pass(): pl.pallas_call(item_kernel, out_shape=(jax.ShapeDtypeStruct((ranks, share...  6.68 us
  transfers between devices with their start and end apart: 4, of which 4 were waited for; matrix products, arithmetic and copies ran while one was open for 0% of the time, Pallas kernels for 0%

profile of v3, /device:TPU:1, one launch (start us, length us, event | category | flops | bytes accessed | tf_op | source)
XLA Modules:
  0.0 126.2 jit_solution(7236088067302215653)
XLA Ops:
  0.6 1.4 %share_items.1 = bf16[24,32,128]{2,1,0:T(8,128)(2,1)} custom-call(f32[32,128]{1,0:T(8,128)} %items.1), custom_call_target="tpu_custom_call" | custom-call | tf_op jit(solution)/shard_map/share_items/pallas_call | solution.py:204
  2.0 20.0 %all-to-all-start = ((bf16[24,32,128]{2,1,0:T(8,128)(2,1)}), bf16[24,32,128]{2,1,0:T(8,128)(2,1)S(1)}, u32[]{:S(2)}, u32[]{:S(2)}) async-start(bf16[24,32,128]{2,1,0:T(8,128)(2,1)} %share_items.1), calls=%async_computation | async-start | bytes 393216 | tf_op jit(solution)/shard_map/all_to_all | solution.py:306
  22.7 11.3 %all-to-all-done = bf16[24,32,128]{2,1,0:T(8,128)(2,1)S(1)} async-done(((bf16[24,32,128]{2,1,0:T(8,128)(2,1)}), bf16[24,32,128]{2,1,0:T(8,128)(2,1)S(1)}, u32[]{:S(2)}, u32[]{:S(2)}) %all-to-all-start) | async-done | bytes 196640 | tf_op jit(solution)/shard_map/all_to_all | solution.py:306
  34.0 3.9 %all-gather = bf16[48,32,128]{2,1,0:T(8,128)(2,1)S(1)} all-gather(bf16[24,32,128]{2,1,0:T(8,128)(2,1)S(1)} %all-to-all-done), channel_id=2, replica_groups=mesh['z_hi'=3,'y'=8,'core'=2,'x'=4,'z_lo'=4] {'core'}, dimensions={0}, use_global_device_ids=true | all-gather | bytes 589824 | tf_op jit(solution)/shard_map/all_gather | solution.py:307
  37.9 0.0 copy-start
  37.9 0.7 copy-done
  38.6 8.4 %user_pass.1 = (bf16[2048,128]{1,0:T(8,128)(2,1)}, bf16[1536,128]{1,0:T(8,128)(2,1)S(1)}, s32[192]{0:T(256)S(1)}) custom-call(s32[128]{0:T(128)S(1)} %bitcast.11, s32[1]{0:T(128)} %bitcast.8.count, f32[2048,128]{1,0:T(8,128)} %parameter.1, bf16[2,24,32,128]{3,2,1,0:T(8,128)(2,1)S(1)} %bitcast.10, bf16[128,128,128]{2,1,0:T(8,128)(2,1)} %bitcast.12), custom_call_target="tpu_custom_call" | custom-call | tf_op jit(solution)/shard_map/user_pass/pallas_call | solution.py:215
  46.9 9.8 %all-to-all-start.1 = ((bf16[16,128,128]{2,1,0:T(8,128)(2,1)}), bf16[16,128,128]{2,1,0:T(8,128)(2,1)S(1)}, u32[]{:S(2)}, u32[]{:S(2)}) async-start(bf16[16,128,128]{2,1,0:T(8,128)(2,1)} %bitcast.5), calls=%async_computation.1 | async-start | bytes 1048576 | tf_op jit(solution)/shard_map/all_to_all | solution.py:312
  56.7 15.8 %all-to-all-done.1.got = bf16[16,128,128]{2,1,0:T(8,128)(2,1)S(1)} async-done(((bf16[16,128,128]{2,1,0:T(8,128)(2,1)}), bf16[16,128,128]{2,1,0:T(8,128)(2,1)S(1)}, u32[]{:S(2)}, u32[]{:S(2)}) %all-to-all-start.1) | async-done | bytes 524320 | tf_op jit(solution)/shard_map/all_to_all | solution.py:312
  72.5 1.9 %user_update.1 = (f32[128,128]{1,0:T(8,128)}, f32[128,128]{1,0:T(8,128)}, f32[128,128]{1,0:T(8,128)}, bf16[16,128,128]{2,1,0:T(8,128)(2,1)}) custom-call(s32[1]{0:T(128)} %bitcast.offset, bf16[16,128,128]{2,1,0:T(8,128)(2,1)S(1)} %all-to-all-done.1.got, f32[2048,128]{1,0:T(8,128)} %parameter.1, f32[2048,128]{1,0:T(8,128)} %first.1, f32[2048,128]{1,0:T(8,128)} %second.1), custom_call_target="tpu_custom_call" | custom-call | tf_op jit(solution)/shard_map/user_update/pallas_call | solution.py:270
  74.4 0.0 copy-start.1
  74.4 0.0 copy-start.2
  74.4 0.0 copy-start.3
  74.4 4.2 %all-to-all-start.2 = ((bf16[16,128,128]{2,1,0:T(8,128)(2,1)}), bf16[16,128,128]{2,1,0:T(8,128)(2,1)S(1)}, u32[]{:S(2)}, u32[]{:S(2)}) async-start(bf16[16,128,128]{2,1,0:T(8,128)(2,1)} %get-tuple-element.20), calls=%async_computation.2 | async-start | bytes 1048576 | tf_op jit(solution)/shard_map/all_to_all | solution.py:316
  78.6 15.8 %all-to-all-done.2 = bf16[16,128,128]{2,1,0:T(8,128)(2,1)S(1)} async-done(((bf16[16,128,128]{2,1,0:T(8,128)(2,1)}), bf16[16,128,128]{2,1,0:T(8,128)(2,1)S(1)}, u32[]{:S(2)}, u32[]{:S(2)}) %all-to-all-start.2) | async-done | bytes 524320 | tf_op jit(solution)/shard_map/all_to_all | solution.py:316
  94.4 6.7 %item_pass.1 = (f32[24,32,128]{2,1,0:T(8,128)S(1)}, bf16[24,32,128]{2,1,0:T(8,128)(2,1)S(1)}) custom-call(s32[1]{0:T(128)} %bitcast.6.core, s32[192]{0:T(256)S(1)} %get-tuple-element.19.places, bf16[2048,128]{1,0:T(8,128)(2,1)S(1)} %bitcast.9, bf16[1536,128]{1,0:T(8,128)(2,1)S(1)} %get-tuple-element.21.items, bf16[128,128,128]{2,1,0:T(8,128)(2,1)} %bitcast.13), custom_call_target="tpu_custom_call" | custom-call | tf_op jit(solution)/shard_map/item_pass/pallas_call | solution.py:244
  101.1 3.6 %collective-permute-start = (bf16[24,32,128]{2,1,0:T(8,128)(2,1)S(1)}, bf16[24,32,128]{2,1,0:T(8,128)(2,1)S(1)}, u32[]{:S(2)}, u32[]{:S(2)}) collective-permute-start(bf16[24,32,128]{2,1,0:T(8,128)(2,1)S(1)} %get-tuple-element.23), channel_id=1, source_target_pairs={{0,16},{16,0},{1,17},{17,1},{2,18},{18,2},{3,19},{19,3},{4,20},{20... | collective-permute-start | bytes 589832 | tf_op jit(solution)/shard_map/ppermute | solution.py:319
  104.7 1.0 collective-permute-done
  105.8 0.1 add_convert_fusion
  105.8 19.6 %all_to_all.20 = bf16[24,32,128]{2,1,0:T(8,128)(2,1)S(1)} all-to-all(bf16[24,32,128]{2,1,0:T(8,128)(2,1)S(1)} %add_convert_fusion), channel_id=1, replica_groups=mesh['z_hi'=3,'y'=8,'core'=2,'x'=4,'z_lo'=4] {'z_hi','y'}, dimensions={0} | all-to-all | bytes 393216 | tf_op jit(solution)/shard_map/all_to_all | solution.py:321
  125.5 0.0 copy-done.1
  125.5 0.0 copy-done.2
  125.5 0.0 copy-done.3
  125.5 0.6 multiply_subtract_fusion
  (1 shorter events, 0.0 us)
Async XLA Ops:
  2.0 31.9 %all-to-all-start = ((bf16[24,32,128]{2,1,0:T(8,128)(2,1)}), bf16[24,32,128]{2,1,0:T(8,128)(2,1)S(1)}, u32[]{:S(2)}, u32[]{:S(2)}) async-start(bf16[24,32,128]{2,1,0:T(8,128)(2,1)} %share_items.1), calls=%async_computation | async-start | bytes 393216 | tf_op jit(solution)/shard_map/all_to_all | solution.py:306
  37.9 0.7 copy-start
  46.9 25.6 %all-to-all-start.1 = ((bf16[16,128,128]{2,1,0:T(8,128)(2,1)}), bf16[16,128,128]{2,1,0:T(8,128)(2,1)S(1)}, u32[]{:S(2)}, u32[]{:S(2)}) async-start(bf16[16,128,128]{2,1,0:T(8,128)(2,1)} %bitcast.5), calls=%async_computation.1 | async-start | bytes 1048576 | tf_op jit(solution)/shard_map/all_to_all | solution.py:312
  74.4 51.1 %copy-start.1 = (f32[32,128]{1,0:T(8,128)S(1)}, f32[32,128]{1,0:T(8,128)}, u32[]{:S(2)}) copy-start(f32[32,128]{1,0:T(8,128)} %items.1) | copy-start | bytes 49156
  74.4 51.1 %copy-start.2 = (f32[32,128]{1,0:T(8,128)S(1)}, f32[32,128]{1,0:T(8,128)}, u32[]{:S(2)}) copy-start(f32[32,128]{1,0:T(8,128)} %param.13) | copy-start | bytes 49156
  74.4 51.1 %copy-start.3 = (f32[32,128]{1,0:T(8,128)S(1)}, f32[32,128]{1,0:T(8,128)}, u32[]{:S(2)}) copy-start(f32[32,128]{1,0:T(8,128)} %param.14) | copy-start | bytes 49156
  74.4 20.0 %all-to-all-start.2 = ((bf16[16,128,128]{2,1,0:T(8,128)(2,1)}), bf16[16,128,128]{2,1,0:T(8,128)(2,1)S(1)}, u32[]{:S(2)}, u32[]{:S(2)}) async-start(bf16[16,128,128]{2,1,0:T(8,128)(2,1)} %get-tuple-element.20), calls=%async_computation.2 | async-start | bytes 1048576 | tf_op jit(solution)/shard_map/all_to_all | solution.py:316
  101.1 4.6 %collective-permute-start = (bf16[24,32,128]{2,1,0:T(8,128)(2,1)S(1)}, bf16[24,32,128]{2,1,0:T(8,128)(2,1)S(1)}, u32[]{:S(2)}, u32[]{:S(2)}) collective-permute-start(bf16[24,32,128]{2,1,0:T(8,128)(2,1)S(1)} %get-tuple-element.23), channel_id=1, source_target_pairs={{0,16},{16,0},{1,17},{17,1},{2,18},{18,2},{3,19},{19,3},{4,20},{20... | collective-permute-start | bytes 589832 | tf_op jit(solution)/shard_map/ppermute | solution.py:319

commit v4 on v3

--- a/solution.py
+++ b/solution.py
@@ -24,6 +24,8 @@
 IBLK = 12
 MAXB = 128
 CHUNK = 8
+USER_PAIRS = 2
+ITEM_PAIRS = 2
 PARTS = ("z_hi", "y", "core", "x", "z_lo")
 USERS = PARTS[:3]
 ITEMS = PARTS[3:]
@@ -63,77 +65,91 @@
     lax.fori_loop(0, (count + CHUNK - 1) // CHUNK, advance, 0)
 
 
-def value_copies(values, buffer, arrivals):
-    return [
-        pltpu.make_async_copy(
-            values.at[pl.ds(chunk * CHUNK, CHUNK)],
-            buffer.at[pl.ds(chunk * CHUNK, CHUNK)],
-            arrivals.at[chunk],
-        )
-        for chunk in range(MAXB // CHUNK)
-    ]
-
-
-def weighted(predicted, place, values):
+def weighted(predicted, place, target):
     live = place < MAXB
     base = jnp.where(live, 1.0, 0.0).astype(jnp.float32)
     slope = jnp.where(live, conf_alpha, 0.0).astype(jnp.float32)
-    target = values[jnp.minimum(place, MAXB - 1)].astype(jnp.float32)
+    target = target.astype(jnp.float32)
     return ((base + slope * target) * (predicted - target)).astype(jnp.bfloat16)
 
 
-def square_error(user_pair, item_pair, first_place, places, values):
+def square_error(user_pair, item_pair, pair, turn, places, buffer):
     predicted = dot_nt(user_pair, item_pair)
     rows = []
     for row in range(2):
         columns = []
         for column in range(2):
             part = predicted[row * EDGE : (row + 1) * EDGE, column * EDGE : (column + 1) * EDGE]
-            columns.append(weighted(part, places[first_place + row * IBLK + column], values))
+            block, item = pair * 2 + row, turn * 2 + column
+            columns.append(weighted(part, places[block * IBLK + item], buffer[block, item]))
         rows.append(jnp.concatenate(columns, axis=1))
     return jnp.concatenate(rows, axis=0)
 
 
-def user_kernel(
-    slots, count, users, gathered, values, out, panel, places_out, places, low, buffer, arrivals, ready
-):
-    copies = value_copies(values, buffer, arrivals)
-    fetch = pltpu.make_async_copy(users, low, ready)
-    fetch.start()
-    for copy in copies:
-        copy.start()
+def open_kernel(slots, count, users, values, low, places_out, dense, places, arrivals):
     fill_places(count[0], slots, places)
+
+    def send(block, carry):
+        for item in range(IBLK):
+            place = jnp.minimum(places[block * IBLK + item], MAXB - 1)
+            pltpu.make_async_copy(
+                values.at[place], dense.at[block, item], arrivals.at[block]
+            ).start()
+        return carry
+
+    lax.fori_loop(0, UBLK, send, 0)
+    low[...] = users[...].astype(jnp.bfloat16)
+    for place in range(UBLK * IBLK):
+        places_out[place] = places[place]
+    for block in range(UBLK):
+        pltpu.make_async_copy(
+            values.at[pl.ds(0, IBLK)], dense.at[block], arrivals.at[block]
+        ).wait()
+
+
+def user_kernel(places, users, gathered, dense, out, panel, turned, buffer, arrivals):
+    def arrival(pair):
+        rows = pl.ds(pair * 2, 2)
+        return pltpu.make_async_copy(dense.at[rows], buffer.at[rows], arrivals.at[pair])
+
+    for pair in range(UBLK // 2):
+        arrival(pair).start()
     share = gathered.shape[2]
     for rank in range(gathered.shape[1]):
         for core in range(2):
             first = (rank * 2 + core) * share
             panel[first : first + share, :] = gathered[core, rank]
-    for place in range(UBLK * IBLK):
-        places_out[place] = places[place]
-    fetch.wait()
-    for copy in copies:
-        copy.wait()
-
-    def advance(pair, carry):
-        rows = pl.ds(pl.multiple_of(pair * 2 * EDGE, 2 * EDGE), 2 * EDGE)
-        user_pair = low[rows, :].astype(jnp.bfloat16)
-        errors = []
-        for turn in range(IBLK // 2):
-            item_pair = panel[turn * 2 * EDGE : (turn + 1) * 2 * EDGE, :]
-            errors.append(
-                square_error(user_pair, item_pair, pair * 2 * IBLK + turn * 2, places, buffer)
-            )
-        total = dot_nn(jnp.concatenate(errors, axis=1), panel[...])
-        out[rows, :] = total.astype(jnp.bfloat16)
+    for block in range(IBLK):
+        span = slice(block * EDGE, (block + 1) * EDGE)
+        turned[:, span] = panel[span, :].T
+
+    def advance(step, carry):
+        for part in range(USER_PAIRS):
+            arrival(step * USER_PAIRS + part).wait()
+        for part in range(USER_PAIRS):
+            pair = step * USER_PAIRS + part
+            rows = pl.ds(pl.multiple_of(pair * 2 * EDGE, 2 * EDGE), 2 * EDGE)
+            user_pair = users[rows, :]
+            errors = []
+            for turn in range(IBLK // 2):
+                item_pair = panel[turn * 2 * EDGE : (turn + 1) * 2 * EDGE, :]
+                errors.append(square_error(user_pair, item_pair, pair, turn, places, buffer))
+            total = dot_nt(turned[...], jnp.concatenate(errors, axis=1))
+            out[rows, :] = total.T.astype(jnp.bfloat16)
         return carry
 
-    lax.fori_loop(0, UBLK // 2, advance, 0, unroll=4)
-
-
-def item_kernel(core, places, users, items, values, keep, sent, turned, buffer, arrivals):
-    copies = value_copies(values, buffer, arrivals)
-    for copy in copies:
-        copy.start()
+    lax.fori_loop(0, UBLK // 2 // USER_PAIRS, advance, 0)
+
+
+def item_kernel(core, places, users, items, dense, keep, sent, turned, buffer, arrivals):
+    def arrival(turn):
+        columns = pl.ds(turn * 2, 2)
+        return pltpu.make_async_copy(
+            dense.at[:, columns], buffer.at[:, columns], arrivals.at[turn]
+        )
+
+    for turn in range(IBLK // 2):
+        arrival(turn).start()
     for block in range(UBLK):
         turned[:, block * EDGE : (block + 1) * EDGE] = users[
             block * EDGE : (block + 1) * EDGE, :
@@ -141,27 +157,27 @@
     share = keep.shape[1]
     ranks = EDGE // share
     first_core = core[0] == 0
-    for copy in copies:
-        copy.wait()
-
-    def advance(turn, carry):
-        rows = pl.ds(pl.multiple_of(turn * 2 * EDGE, 2 * EDGE), 2 * EDGE)
-        item_pair = items[rows, :]
-        errors = []
-        for pair in range(UBLK // 2):
-            span = slice(pair * 2 * EDGE, (pair + 1) * 2 * EDGE)
-            errors.append(
-                square_error(users[span, :], item_pair, pair * 2 * IBLK + turn * 2, places, buffer)
-            )
-        running = dot_nn(turned[...], jnp.concatenate(errors, axis=0))
-        split = running.T.reshape(ranks, 2, share, RANK)
-        even, odd = split[:, 0], split[:, 1]
-        where = pl.ds(turn * ranks, ranks)
-        keep[where] = jnp.where(first_core, even, odd)
-        sent[where] = jnp.where(first_core, odd, even).astype(jnp.bfloat16)
+
+    def advance(step, carry):
+        for part in range(ITEM_PAIRS):
+            arrival(step * ITEM_PAIRS + part).wait()
+        for part in range(ITEM_PAIRS):
+            turn = step * ITEM_PAIRS + part
+            rows = pl.ds(pl.multiple_of(turn * 2 * EDGE, 2 * EDGE), 2 * EDGE)
+            item_pair = items[rows, :]
+            errors = []
+            for pair in range(UBLK // 2):
+                span = slice(pair * 2 * EDGE, (pair + 1) * 2 * EDGE)
+                errors.append(square_error(users[span, :], item_pair, pair, turn, places, buffer))
+            running = dot_nn(turned[...], jnp.concatenate(errors, axis=0))
+            split = running.T.reshape(ranks, 2, share, RANK)
+            even, odd = split[:, 0], split[:, 1]
+            where = pl.ds(turn * ranks, ranks)
+            keep[where] = jnp.where(first_core, even, odd)
+            sent[where] = jnp.where(first_core, odd, even).astype(jnp.bfloat16)
         return carry
 
-    lax.fori_loop(0, IBLK // 2, advance, 0, unroll=3)
+    lax.fori_loop(0, IBLK // 2 // ITEM_PAIRS, advance, 0)
 
 
 def user_update_kernel(
@@ -210,36 +226,50 @@
     )(items)
 
 
-def user_pass(slots, count, users, gathered, values):
+SCALAR = whole(pltpu.SMEM)
+VECTOR = whole(pltpu.VMEM)
+DISTANT = whole(pltpu.HBM)
+
+
+def open_pass(slots, count, users, values):
+    return pl.pallas_call(
+        open_kernel,
+        out_shape=(
+            jax.ShapeDtypeStruct((UBLK * EDGE, RANK), jnp.bfloat16),
+            jax.ShapeDtypeStruct((UBLK * IBLK,), jnp.int32),
+            jax.ShapeDtypeStruct((UBLK, IBLK, EDGE, EDGE), jnp.bfloat16),
+        ),
+        in_specs=[SCALAR, SCALAR, VECTOR, DISTANT],
+        out_specs=(VECTOR, SCALAR, DISTANT),
+        scratch_shapes=[
+            pltpu.SMEM((UBLK * IBLK,), jnp.int32),
+            pltpu.SemaphoreType.DMA((UBLK,)),
+        ],
+        name="open_pass",
+    )(slots, count, users, values)
+
+
+def user_pass(places, users, gathered, dense):
     panel = (gathered.shape[0] * gathered.shape[1] * gathered.shape[2], RANK)
     return pl.pallas_call(
         user_kernel,
         out_shape=(
             jax.ShapeDtypeStruct((UBLK * EDGE, RANK), jnp.bfloat16),
             jax.ShapeDtypeStruct(panel, jnp.bfloat16),
-            jax.ShapeDtypeStruct((UBLK * IBLK,), jnp.int32),
-        ),
-        in_specs=[
-            whole(pltpu.SMEM),
-            whole(pltpu.SMEM),
-            whole(pltpu.HBM),
-            whole(pltpu.VMEM),
-            whole(pltpu.HBM),
+        ),
+        in_specs=[SCALAR, VECTOR, VECTOR, DISTANT],
+        out_specs=(VECTOR, VECTOR),
+        scratch_shapes=[
+            pltpu.VMEM((RANK, IBLK * EDGE), jnp.bfloat16),
+            pltpu.VMEM((UBLK, IBLK, EDGE, EDGE), jnp.bfloat16),
+            pltpu.SemaphoreType.DMA((UBLK // 2,)),
         ],
-        out_specs=(whole(pltpu.VMEM), whole(pltpu.VMEM), whole(pltpu.SMEM)),
-        scratch_shapes=[
-            pltpu.SMEM((UBLK * IBLK,), jnp.int32),
-            pltpu.VMEM((UBLK * EDGE, RANK), jnp.float32),
-            pltpu.VMEM((MAXB, EDGE, EDGE), jnp.bfloat16),
-            pltpu.SemaphoreType.DMA((MAXB // CHUNK,)),
-            pltpu.SemaphoreType.DMA,
-        ],
-        compiler_params=grant(16),
+        compiler_params=grant(20),
         name="user_pass",
-    )(slots, count, users, gathered, values)
-
-
-def item_pass(core, places, users, items, values, share):
+    )(places, users, gathered, dense)
+
+
+def item_pass(core, places, users, items, dense, share):
     ranks = items.shape[0] // (2 * share)
     return pl.pallas_call(
         item_kernel,
@@ -247,22 +277,16 @@
             jax.ShapeDtypeStruct((ranks, share, RANK), jnp.float32),
             jax.ShapeDtypeStruct((ranks, share, RANK), jnp.bfloat16),
         ),
-        in_specs=[
-            whole(pltpu.SMEM),
-            whole(pltpu.SMEM),
-            whole(pltpu.VMEM),
-            whole(pltpu.VMEM),
-            whole(pltpu.HBM),
-        ],
-        out_specs=(whole(pltpu.VMEM), whole(pltpu.VMEM)),
+        in_specs=[SCALAR, SCALAR, VECTOR, VECTOR, DISTANT],
+        out_specs=(VECTOR, VECTOR),
         scratch_shapes=[
             pltpu.VMEM((RANK, UBLK * EDGE), jnp.bfloat16),
-            pltpu.VMEM((MAXB, EDGE, EDGE), jnp.bfloat16),
-            pltpu.SemaphoreType.DMA((MAXB // CHUNK,)),
+            pltpu.VMEM((UBLK, IBLK, EDGE, EDGE), jnp.bfloat16),
+            pltpu.SemaphoreType.DMA((IBLK // 2,)),
         ],
-        compiler_params=grant(16),
+        compiler_params=grant(20),
         name="item_pass",
-    )(core, places, users, items, values)
+    )(core, places, users, items, dense)
 
 
 def user_update(offset, got, parameter, first, second, scale):
@@ -296,7 +320,7 @@
     block_count,
     block_values,
 ):
-    slots = block_slot.reshape(MAXB)
+    slots = far(block_slot.reshape(MAXB))
     count = block_count.reshape(1)
     values = far(block_values.reshape(MAXB, EDGE, EDGE))
     user_state = [far(array) for array in (user_factors, user_moment_one, user_moment_two)]
@@ -304,8 +328,9 @@
     user_total = user_factors.shape[0] * lax.axis_size(USERS)
     shared = share_items(item_factors, lax.axis_size(("z_hi", "y")))
     half = lax.all_to_all(shared, ("z_hi", "y"), 0, 0)
+    user_low, places, dense = open_pass(slots, count, user_factors, values)
     gathered = lax.all_gather(half, "core", axis=0)
-    user_partial, items, places = user_pass(slots, count, user_state[0], gathered, values)
+    user_partial, items = user_pass(far(places), far(user_low), gathered, far(dense))
     user_share = user_factors.shape[0] // lax.axis_size(ITEMS)
     user_offset = lax.axis_index(ITEMS) * user_share
     sent = user_partial.reshape(-1, user_share, RANK)
@@ -315,7 +340,7 @@
     )
     new_low = lax.all_to_all(shared, ITEMS, 0, 0).reshape(-1, RANK)
     core = lax.axis_index("core").reshape(1)
-    keep, sent = item_pass(core, places, new_low, items, values, item_factors.shape[0])
+    keep, sent = item_pass(core, far(places), new_low, items, far(dense), item_factors.shape[0])
     other = lax.ppermute(sent, "core", [(0, 1), (1, 0)])
     both = (keep + other.astype(jnp.float32)).astype(jnp.bfloat16)
     got = lax.all_to_all(both, ("z_hi", "y"), 0, 0)

time: 127 us -> 311 us (2.45)
  Pallas kernels: 18.3 us -> 212 us
  waiting for transfers between devices: 43.9 us -> 32.6 us
  blocking collectives: 23.6 us -> 29.5 us
    pallas_call x0 -> x1, Pallas kernels: none -> 194 us  [open_pass(): pl.pallas_call(open_kernel, out_shape=(jax.ShapeDtypeStruct((UBLK * EDGE,...]
    all_to_all x1, waiting for transfers between devices: 11.3 us -> 0.01 us  [on_device(): half = lax.all_to_all(shared, ('z_hi', 'y'), 0, 0)]
    all_to_all x1, blocking collectives: 19.6 us -> 26.8 us  [on_device(): got = lax.all_to_all(both, ('z_hi', 'y'), 0, 0)]
  transfers between devices with their start and end apart: 4 -> 4, of which waited for: 4 -> 3; matrix products, arithmetic and copies ran while one was open for 0% -> 0% of each run, Pallas kernels for 0% -> 62%
where the time goes in v4:
time: 311 us
  Pallas kernels  212 us (68%)
  starting transfers between devices  34.5 us (11%)
  waiting for transfers between devices  32.6 us (10%)
  blocking collectives  29.5 us (9%)
    pallas_call x1, Pallas kernels, open_pass(): pl.pallas_call(open_kernel, out_shape=(jax.ShapeDtypeStruct((UBLK * EDGE,...  194 us
    all_to_all x1, blocking collectives, on_device(): got = lax.all_to_all(both, ('z_hi', 'y'), 0, 0)  26.8 us
    all_to_all x1, starting transfers between devices, on_device(): half = lax.all_to_all(shared, ('z_hi', 'y'), 0, 0)  20 us
    all_to_all x1, waiting for transfers between devices, on_device(): new_low = lax.all_to_all(shared, ITEMS, 0, 0).reshape(-1, RANK)  15.8 us
    all_to_all x1, waiting for transfers between devices, on_device(): got = lax.all_to_all(sent, ITEMS, 0, 0)  15.8 us
    pallas_call x1, Pallas kernels, user_pass(): pl.pallas_call(user_kernel, out_shape=(jax.ShapeDtypeStruct((UBLK * EDGE,...  8.21 us
    all_to_all x1, starting transfers between devices, on_device(): got = lax.all_to_all(sent, ITEMS, 0, 0)  6.86 us
  transfers between devices with their start and end apart: 4, of which 3 were waited for; matrix products, arithmetic and copies ran while one was open for 0% of the time, Pallas kernels for 62%

profile of v4, /device:TPU:1, one launch (start us, length us, event | category | flops | bytes accessed | tf_op | source)
XLA Modules:
  0.0 310.6 jit_solution(15636968580992048107)
XLA Ops:
  0.6 1.4 share_items.1
  2.0 20.0 %all-to-all-start = ((bf16[24,32,128]{2,1,0:T(8,128)(2,1)}), bf16[24,32,128]{2,1,0:T(8,128)(2,1)S(1)}, u32[]{:S(2)}, u32[]{:S(2)}) async-start(bf16[24,32,128]{2,1,0:T(8,128)(2,1)} %share_items.1), calls=%async_computation | async-start | bytes 393216 | tf_op jit(solution)/shard_map/all_to_all | solution.py:330
  22.7 194.1 %open_pass.1 = (bf16[2048,128]{1,0:T(8,128)(2,1)}, s32[192]{0:T(256)}, bf16[16,12,128,128]{3,2,1,0:T(8,128)(2,1)}) custom-call(s32[128]{0:T(128)} %bitcast.12, s32[1]{0:T(128)} %bitcast.8.count, f32[2048,128]{1,0:T(8,128)} %parameter.1, bf16[128,128,128]{2,1,0:T(8,128)(2,1)} %bitcast.11), custom_call_target="tpu_custom_call" | custom-call | tf_op jit(solution)/shard_map/open_pass/pallas_call | solution.py:235
  216.8 0.0 all-to-all-done
  216.8 2.7 all-gather
  219.5 8.2 %user_pass.1 = (bf16[2048,128]{1,0:T(8,128)(2,1)}, bf16[1536,128]{1,0:T(8,128)(2,1)S(1)}) custom-call(s32[192]{0:T(256)} %get-tuple-element.17.places, bf16[2048,128]{1,0:T(8,128)(2,1)} %get-tuple-element.18.users, bf16[2,24,32,128]{3,2,1,0:T(8,128)(2,1)S(1)} %bitcast.10, bf16[16,12,128,128]{3,2,1,0:T(8,128)(2,1)} %get-tuple-element.19.dense), custom_call_target="tpu_custom_call" | custom-call | tf_op jit(solution)/shard_map/user_pass/pallas_call | solution.py:254
  227.7 6.9 %all-to-all-start.1 = ((bf16[16,128,128]{2,1,0:T(8,128)(2,1)}), bf16[16,128,128]{2,1,0:T(8,128)(2,1)S(1)}, u32[]{:S(2)}, u32[]{:S(2)}) async-start(bf16[16,128,128]{2,1,0:T(8,128)(2,1)} %bitcast.5), calls=%async_computation.1 | async-start | bytes 1048576 | tf_op jit(solution)/shard_map/all_to_all | solution.py:337
  234.6 15.8 %all-to-all-done.1.got = bf16[16,128,128]{2,1,0:T(8,128)(2,1)S(1)} async-done(((bf16[16,128,128]{2,1,0:T(8,128)(2,1)}), bf16[16,128,128]{2,1,0:T(8,128)(2,1)S(1)}, u32[]{:S(2)}, u32[]{:S(2)}) %all-to-all-start.1) | async-done | bytes 524320 | tf_op jit(solution)/shard_map/all_to_all | solution.py:337
  250.4 0.0 copy-start
  250.4 0.0 copy-start.1
  250.4 0.0 copy-start.2
  250.4 1.9 user_update.1
  252.3 4.1 %all-to-all-start.2 = ((bf16[16,128,128]{2,1,0:T(8,128)(2,1)}), bf16[16,128,128]{2,1,0:T(8,128)(2,1)S(1)}, u32[]{:S(2)}, u32[]{:S(2)}) async-start(bf16[16,128,128]{2,1,0:T(8,128)(2,1)} %get-tuple-element.24), calls=%async_computation.2 | async-start | bytes 1048576 | tf_op jit(solution)/shard_map/all_to_all | solution.py:341
  256.4 15.8 %all-to-all-done.2 = bf16[16,128,128]{2,1,0:T(8,128)(2,1)S(1)} async-done(((bf16[16,128,128]{2,1,0:T(8,128)(2,1)}), bf16[16,128,128]{2,1,0:T(8,128)(2,1)S(1)}, u32[]{:S(2)}, u32[]{:S(2)}) %all-to-all-start.2) | async-done | bytes 524320 | tf_op jit(solution)/shard_map/all_to_all | solution.py:341
  272.2 6.2 %item_pass.1 = (f32[24,32,128]{2,1,0:T(8,128)S(1)}, bf16[24,32,128]{2,1,0:T(8,128)(2,1)S(1)}) custom-call(s32[1]{0:T(128)} %bitcast.6.core, s32[192]{0:T(256)} %get-tuple-element.17.places, bf16[2048,128]{1,0:T(8,128)(2,1)S(1)} %bitcast.9, bf16[1536,128]{1,0:T(8,128)(2,1)S(1)} %get-tuple-element.25.items, bf16[16,12,128,128]{3,2,1,0:T(8,128)(2,1)} %get-tuple-element.19.dense), custom_call_target="tpu_custom_call" | custom-call | tf_op jit(solution)/shard_map/item_pass/pallas_call | solution.py:274
  278.3 3.6 %collective-permute-start = (bf16[24,32,128]{2,1,0:T(8,128)(2,1)S(1)}, bf16[24,32,128]{2,1,0:T(8,128)(2,1)S(1)}, u32[]{:S(2)}, u32[]{:S(2)}) collective-permute-start(bf16[24,32,128]{2,1,0:T(8,128)(2,1)S(1)} %get-tuple-element.27), channel_id=1, source_target_pairs={{0,16},{16,0},{1,17},{17,1},{2,18},{18,2},{3,19},{19,3},{4,20},{20... | collective-permute-start | bytes 589832 | tf_op jit(solution)/shard_map/ppermute | solution.py:344
  281.9 1.0 collective-permute-done
  283.0 0.1 add_convert_fusion
  283.1 26.8 %all_to_all.20 = bf16[24,32,128]{2,1,0:T(8,128)(2,1)S(1)} all-to-all(bf16[24,32,128]{2,1,0:T(8,128)(2,1)S(1)} %add_convert_fusion), channel_id=1, replica_groups=mesh['z_hi'=3,'y'=8,'core'=2,'x'=4,'z_lo'=4] {'z_hi','y'}, dimensions={0} | all-to-all | bytes 393216 | tf_op jit(solution)/shard_map/all_to_all | solution.py:346
  309.9 0.0 copy-done
  309.9 0.0 copy-done.1
  309.9 0.0 copy-done.2
  309.9 0.6 multiply_subtract_fusion
  (1 shorter events, 0.0 us)
Async XLA Ops:
  2.0 214.7 %all-to-all-start = ((bf16[24,32,128]{2,1,0:T(8,128)(2,1)}), bf16[24,32,128]{2,1,0:T(8,128)(2,1)S(1)}, u32[]{:S(2)}, u32[]{:S(2)}) async-start(bf16[24,32,128]{2,1,0:T(8,128)(2,1)} %share_items.1), calls=%async_computation | async-start | bytes 393216 | tf_op jit(solution)/shard_map/all_to_all | solution.py:330
  227.7 22.6 %all-to-all-start.1 = ((bf16[16,128,128]{2,1,0:T(8,128)(2,1)}), bf16[16,128,128]{2,1,0:T(8,128)(2,1)S(1)}, u32[]{:S(2)}, u32[]{:S(2)}) async-start(bf16[16,128,128]{2,1,0:T(8,128)(2,1)} %bitcast.5), calls=%async_computation.1 | async-start | bytes 1048576 | tf_op jit(solution)/shard_map/all_to_all | solution.py:337
  250.4 59.5 %copy-start = (f32[32,128]{1,0:T(8,128)S(1)}, f32[32,128]{1,0:T(8,128)}, u32[]{:S(2)}) copy-start(f32[32,128]{1,0:T(8,128)} %items.1) | copy-start | bytes 49156
  250.4 59.5 %copy-start.1 = (f32[32,128]{1,0:T(8,128)S(1)}, f32[32,128]{1,0:T(8,128)}, u32[]{:S(2)}) copy-start(f32[32,128]{1,0:T(8,128)} %param.13) | copy-start | bytes 49156
  250.4 59.5 %copy-start.2 = (f32[32,128]{1,0:T(8,128)S(1)}, f32[32,128]{1,0:T(8,128)}, u32[]{:S(2)}) copy-start(f32[32,128]{1,0:T(8,128)} %param.14) | copy-start | bytes 49156
  252.3 19.9 %all-to-all-start.2 = ((bf16[16,128,128]{2,1,0:T(8,128)(2,1)}), bf16[16,128,128]{2,1,0:T(8,128)(2,1)S(1)}, u32[]{:S(2)}, u32[]{:S(2)}) async-start(bf16[16,128,128]{2,1,0:T(8,128)(2,1)} %get-tuple-element.24), calls=%async_computation.2 | async-start | bytes 1048576 | tf_op jit(solution)/shard_map/all_to_all | solution.py:341
  278.3 4.7 %collective-permute-start = (bf16[24,32,128]{2,1,0:T(8,128)(2,1)S(1)}, bf16[24,32,128]{2,1,0:T(8,128)(2,1)S(1)}, u32[]{:S(2)}, u32[]{:S(2)}) collective-permute-start(bf16[24,32,128]{2,1,0:T(8,128)(2,1)S(1)} %get-tuple-element.27), channel_id=1, source_target_pairs={{0,16},{16,0},{1,17},{17,1},{2,18},{18,2},{3,19},{19,3},{4,20},{20... | collective-permute-start | bytes 589832 | tf_op jit(solution)/shard_map/ppermute | solution.py:344

commit v5 on v4

--- a/solution.py
+++ b/solution.py
@@ -107,7 +107,7 @@
         ).wait()
 
 
-def user_kernel(places, users, gathered, dense, out, panel, turned, buffer, arrivals):
+def user_kernel(places, users, gathered, dense, out, panel, buffer, arrivals):
     def arrival(pair):
         rows = pl.ds(pair * 2, 2)
         return pltpu.make_async_copy(dense.at[rows], buffer.at[rows], arrivals.at[pair])
@@ -119,9 +119,6 @@
         for core in range(2):
             first = (rank * 2 + core) * share
             panel[first : first + share, :] = gathered[core, rank]
-    for block in range(IBLK):
-        span = slice(block * EDGE, (block + 1) * EDGE)
-        turned[:, span] = panel[span, :].T
 
     def advance(step, carry):
         for part in range(USER_PAIRS):
@@ -134,8 +131,8 @@
             for turn in range(IBLK // 2):
                 item_pair = panel[turn * 2 * EDGE : (turn + 1) * 2 * EDGE, :]
                 errors.append(square_error(user_pair, item_pair, pair, turn, places, buffer))
-            total = dot_nt(turned[...], jnp.concatenate(errors, axis=1))
-            out[rows, :] = total.T.astype(jnp.bfloat16)
+            total = dot_nn(jnp.concatenate(errors, axis=1), panel[...])
+            out[rows, :] = total.astype(jnp.bfloat16)
         return carry
 
     lax.fori_loop(0, UBLK // 2 // USER_PAIRS, advance, 0)
@@ -240,7 +237,7 @@
             jax.ShapeDtypeStruct((UBLK, IBLK, EDGE, EDGE), jnp.bfloat16),
         ),
         in_specs=[SCALAR, SCALAR, VECTOR, DISTANT],
-        out_specs=(VECTOR, SCALAR, DISTANT),
+        out_specs=(VECTOR, SCALAR, VECTOR),
         scratch_shapes=[
             pltpu.SMEM((UBLK * IBLK,), jnp.int32),
             pltpu.SemaphoreType.DMA((UBLK,)),
@@ -260,7 +257,6 @@
         in_specs=[SCALAR, VECTOR, VECTOR, DISTANT],
         out_specs=(VECTOR, VECTOR),
         scratch_shapes=[
-            pltpu.VMEM((RANK, IBLK * EDGE), jnp.bfloat16),
             pltpu.VMEM((UBLK, IBLK, EDGE, EDGE), jnp.bfloat16),
             pltpu.SemaphoreType.DMA((UBLK // 2,)),
         ],

time: 311 us -> 127 us (0.41)
  Pallas kernels: 212 us -> 27.7 us
  blocking collectives: 29.5 us -> 25.7 us
    pallas_call x1, Pallas kernels: 194 us -> 10.5 us  [open_pass(): pl.pallas_call(open_kernel, out_shape=(jax.ShapeDtypeStruct((UBLK * EDGE,...]
    all_to_all x1, blocking collectives: 26.8 us -> 21.7 us  [on_device(): got = lax.all_to_all(both, ('z_hi', 'y'), 0, 0)]
  transfers between devices with their start and end apart: 4 -> 4, of which waited for: 3 -> 4; matrix products, arithmetic and copies ran while one was open for 0% -> 0% of each run, Pallas kernels for 62% -> 8%
where the time goes in v5:
time: 127 us; the launch traced here: 126 us
  starting transfers between devices  37.4 us (29%)
  waiting for transfers between devices  33.4 us (26%)
  Pallas kernels  27.7 us (22%)
  blocking collectives  25.7 us (20%)
  between operations  1.38 us (1%)
    all_to_all x1, blocking collectives, on_device(): got = lax.all_to_all(both, ('z_hi', 'y'), 0, 0)  21.7 us
    all_to_all x1, starting transfers between devices, on_device(): half = lax.all_to_all(shared, ('z_hi', 'y'), 0, 0)  20 us
    all_to_all x1, waiting for transfers between devices, on_device(): new_low = lax.all_to_all(shared, ITEMS, 0, 0).reshape(-1, RANK)  15.8 us
    all_to_all x1, waiting for transfers between devices, on_device(): got = lax.all_to_all(sent, ITEMS, 0, 0)  15.8 us
    pallas_call x1, Pallas kernels, open_pass(): pl.pallas_call(open_kernel, out_shape=(jax.ShapeDtypeStruct((UBLK * EDGE,...  10.5 us
    all_to_all x1, starting transfers between devices, on_device(): got = lax.all_to_all(sent, ITEMS, 0, 0)  9.77 us
    pallas_call x1, Pallas kernels, user_pass(): pl.pallas_call(user_kernel, out_shape=(jax.ShapeDtypeStruct((UBLK * EDGE,...  7.76 us
    pallas_call x1, Pallas kernels, item_pass(): pl.pallas_call(item_kernel, out_shape=(jax.ShapeDtypeStruct((ranks, share...  6.17 us
  transfers between devices with their start and end apart: 4, of which 4 were waited for; matrix products, arithmetic and copies ran while one was open for 0% of the time, Pallas kernels for 8%

profile of v5, /device:TPU:1, one launch (start us, length us, event | category | flops | bytes accessed | tf_op | source)
XLA Modules:
  0.0 126.3 jit_solution(3817186576298883898)
XLA Ops:
  0.6 1.4 %share_items.1 = bf16[24,32,128]{2,1,0:T(8,128)(2,1)} custom-call(f32[32,128]{1,0:T(8,128)} %items.1), custom_call_target="tpu_custom_call" | custom-call | tf_op jit(solution)/shard_map/share_items/pallas_call | solution.py:217
  2.0 20.0 %all-to-all-start = ((bf16[24,32,128]{2,1,0:T(8,128)(2,1)}), bf16[24,32,128]{2,1,0:T(8,128)(2,1)S(1)}, u32[]{:S(2)}, u32[]{:S(2)}) async-start(bf16[24,32,128]{2,1,0:T(8,128)(2,1)} %share_items.1), calls=%async_computation | async-start | bytes 393216 | tf_op jit(solution)/shard_map/all_to_all | solution.py:326
  22.7 10.5 %open_pass.1 = (bf16[2048,128]{1,0:T(8,128)(2,1)}, s32[192]{0:T(256)}, bf16[16,12,128,128]{3,2,1,0:T(8,128)(2,1)}) custom-call(s32[128]{0:T(128)} %bitcast.12, s32[1]{0:T(128)} %bitcast.8.count, f32[2048,128]{1,0:T(8,128)} %parameter.1, bf16[128,128,128]{2,1,0:T(8,128)(2,1)} %bitcast.11), custom_call_target="tpu_custom_call" | custom-call | tf_op jit(solution)/shard_map/open_pass/pallas_call | solution.py:232
  33.1 0.8 all-to-all-done
  34.0 3.9 %all-gather = bf16[48,32,128]{2,1,0:T(8,128)(2,1)S(1)} all-gather(bf16[24,32,128]{2,1,0:T(8,128)(2,1)S(1)} %all-to-all-done), channel_id=2, replica_groups=mesh['z_hi'=3,'y'=8,'core'=2,'x'=4,'z_lo'=4] {'core'}, dimensions={0}, use_global_device_ids=true | all-gather | bytes 589824 | tf_op jit(solution)/shard_map/all_gather | solution.py:328
  37.9 7.8 %user_pass.1 = (bf16[2048,128]{1,0:T(8,128)(2,1)}, bf16[1536,128]{1,0:T(8,128)(2,1)S(1)}) custom-call(s32[192]{0:T(256)} %get-tuple-element.17.places, bf16[2048,128]{1,0:T(8,128)(2,1)} %get-tuple-element.18.users, bf16[2,24,32,128]{3,2,1,0:T(8,128)(2,1)S(1)} %bitcast.10, bf16[16,12,128,128]{3,2,1,0:T(8,128)(2,1)} %get-tuple-element.19.dense), custom_call_target="tpu_custom_call" | custom-call | tf_op jit(solution)/shard_map/user_pass/pallas_call | solution.py:251
  45.7 9.8 %all-to-all-start.1 = ((bf16[16,128,128]{2,1,0:T(8,128)(2,1)}), bf16[16,128,128]{2,1,0:T(8,128)(2,1)S(1)}, u32[]{:S(2)}, u32[]{:S(2)}) async-start(bf16[16,128,128]{2,1,0:T(8,128)(2,1)} %bitcast.5), calls=%async_computation.1 | async-start | bytes 1048576 | tf_op jit(solution)/shard_map/all_to_all | solution.py:333
  55.5 15.8 %all-to-all-done.1.got = bf16[16,128,128]{2,1,0:T(8,128)(2,1)S(1)} async-done(((bf16[16,128,128]{2,1,0:T(8,128)(2,1)}), bf16[16,128,128]{2,1,0:T(8,128)(2,1)S(1)}, u32[]{:S(2)}, u32[]{:S(2)}) %all-to-all-start.1) | async-done | bytes 524320 | tf_op jit(solution)/shard_map/all_to_all | solution.py:333
  71.2 0.0 copy-start
  71.2 0.0 copy-start.1
  71.2 0.0 copy-start.2
  71.2 1.9 %user_update.1 = (f32[128,128]{1,0:T(8,128)}, f32[128,128]{1,0:T(8,128)}, f32[128,128]{1,0:T(8,128)}, bf16[16,128,128]{2,1,0:T(8,128)(2,1)}) custom-call(s32[1]{0:T(128)} %bitcast.offset, bf16[16,128,128]{2,1,0:T(8,128)(2,1)S(1)} %all-to-all-done.1.got, f32[2048,128]{1,0:T(8,128)} %parameter.1, f32[2048,128]{1,0:T(8,128)} %first.1, f32[2048,128]{1,0:T(8,128)} %second.1), custom_call_target="tpu_custom_call" | custom-call | tf_op jit(solution)/shard_map/user_update/pallas_call | solution.py:290
  73.1 4.1 %all-to-all-start.2 = ((bf16[16,128,128]{2,1,0:T(8,128)(2,1)}), bf16[16,128,128]{2,1,0:T(8,128)(2,1)S(1)}, u32[]{:S(2)}, u32[]{:S(2)}) async-start(bf16[16,128,128]{2,1,0:T(8,128)(2,1)} %get-tuple-element.24), calls=%async_computation.2 | async-start | bytes 1048576 | tf_op jit(solution)/shard_map/all_to_all | solution.py:337
  77.2 15.8 %all-to-all-done.2 = bf16[16,128,128]{2,1,0:T(8,128)(2,1)S(1)} async-done(((bf16[16,128,128]{2,1,0:T(8,128)(2,1)}), bf16[16,128,128]{2,1,0:T(8,128)(2,1)S(1)}, u32[]{:S(2)}, u32[]{:S(2)}) %all-to-all-start.2) | async-done | bytes 524320 | tf_op jit(solution)/shard_map/all_to_all | solution.py:337
  93.0 6.2 %item_pass.1 = (f32[24,32,128]{2,1,0:T(8,128)S(1)}, bf16[24,32,128]{2,1,0:T(8,128)(2,1)S(1)}) custom-call(s32[1]{0:T(128)} %bitcast.6.core, s32[192]{0:T(256)} %get-tuple-element.17.places, bf16[2048,128]{1,0:T(8,128)(2,1)S(1)} %bitcast.9, bf16[1536,128]{1,0:T(8,128)(2,1)S(1)} %get-tuple-element.25.items, bf16[16,12,128,128]{3,2,1,0:T(8,128)(2,1)} %get-tuple-element.19.dense), custom_call_target="tpu_custom_call" | custom-call | tf_op jit(solution)/shard_map/item_pass/pallas_call | solution.py:270
  99.2 3.6 %collective-permute-start = (bf16[24,32,128]{2,1,0:T(8,128)(2,1)S(1)}, bf16[24,32,128]{2,1,0:T(8,128)(2,1)S(1)}, u32[]{:S(2)}, u32[]{:S(2)}) collective-permute-start(bf16[24,32,128]{2,1,0:T(8,128)(2,1)S(1)} %get-tuple-element.27), channel_id=1, source_target_pairs={{0,16},{16,0},{1,17},{17,1},{2,18},{18,2},{3,19},{19,3},{4,20},{20... | collective-permute-start | bytes 589832 | tf_op jit(solution)/shard_map/ppermute | solution.py:340
  102.8 1.0 collective-permute-done
  103.8 0.1 add_convert_fusion
  103.9 21.7 %all_to_all.20 = bf16[24,32,128]{2,1,0:T(8,128)(2,1)S(1)} all-to-all(bf16[24,32,128]{2,1,0:T(8,128)(2,1)S(1)} %add_convert_fusion), channel_id=1, replica_groups=mesh['z_hi'=3,'y'=8,'core'=2,'x'=4,'z_lo'=4] {'z_hi','y'}, dimensions={0} | all-to-all | bytes 393216 | tf_op jit(solution)/shard_map/all_to_all | solution.py:342
  125.7 0.0 copy-done
  125.7 0.0 copy-done.1
  125.7 0.0 copy-done.2
  125.7 0.6 multiply_subtract_fusion
  (1 shorter events, 0.0 us)
Async XLA Ops:
  2.0 31.9 %all-to-all-start = ((bf16[24,32,128]{2,1,0:T(8,128)(2,1)}), bf16[24,32,128]{2,1,0:T(8,128)(2,1)S(1)}, u32[]{:S(2)}, u32[]{:S(2)}) async-start(bf16[24,32,128]{2,1,0:T(8,128)(2,1)} %share_items.1), calls=%async_computation | async-start | bytes 393216 | tf_op jit(solution)/shard_map/all_to_all | solution.py:326
  45.7 25.5 %all-to-all-start.1 = ((bf16[16,128,128]{2,1,0:T(8,128)(2,1)}), bf16[16,128,128]{2,1,0:T(8,128)(2,1)S(1)}, u32[]{:S(2)}, u32[]{:S(2)}) async-start(bf16[16,128,128]{2,1,0:T(8,128)(2,1)} %bitcast.5), calls=%async_computation.1 | async-start | bytes 1048576 | tf_op jit(solution)/shard_map/all_to_all | solution.py:333
  71.2 54.4 %copy-start = (f32[32,128]{1,0:T(8,128)S(1)}, f32[32,128]{1,0:T(8,128)}, u32[]{:S(2)}) copy-start(f32[32,128]{1,0:T(8,128)} %items.1) | copy-start | bytes 49156
  71.2 54.5 %copy-start.1 = (f32[32,128]{1,0:T(8,128)S(1)}, f32[32,128]{1,0:T(8,128)}, u32[]{:S(2)}) copy-start(f32[32,128]{1,0:T(8,128)} %param.13) | copy-start | bytes 49156
  71.2 54.5 %copy-start.2 = (f32[32,128]{1,0:T(8,128)S(1)}, f32[32,128]{1,0:T(8,128)}, u32[]{:S(2)}) copy-start(f32[32,128]{1,0:T(8,128)} %param.14) | copy-start | bytes 49156
  73.1 19.9 %all-to-all-start.2 = ((bf16[16,128,128]{2,1,0:T(8,128)(2,1)}), bf16[16,128,128]{2,1,0:T(8,128)(2,1)S(1)}, u32[]{:S(2)}, u32[]{:S(2)}) async-start(bf16[16,128,128]{2,1,0:T(8,128)(2,1)} %get-tuple-element.24), calls=%async_computation.2 | async-start | bytes 1048576 | tf_op jit(solution)/shard_map/all_to_all | solution.py:337
  99.2 4.7 %collective-permute-start = (bf16[24,32,128]{2,1,0:T(8,128)(2,1)S(1)}, bf16[24,32,128]{2,1,0:T(8,128)(2,1)S(1)}, u32[]{:S(2)}, u32[]{:S(2)}) collective-permute-start(bf16[24,32,128]{2,1,0:T(8,128)(2,1)S(1)} %get-tuple-element.27), channel_id=1, source_target_pairs={{0,16},{16,0},{1,17},{17,1},{2,18},{18,2},{3,19},{19,3},{4,20},{20... | collective-permute-start | bytes 589832 | tf_op jit(solution)/shard_map/ppermute | solution.py:340

commit v6 on v3

--- a/solution.py
+++ b/solution.py
@@ -296,7 +296,7 @@
     block_count,
     block_values,
 ):
-    slots = block_slot.reshape(MAXB)
+    slots = far(block_slot.reshape(MAXB))
     count = block_count.reshape(1)
     values = far(block_values.reshape(MAXB, EDGE, EDGE))
     user_state = [far(array) for array in (user_factors, user_moment_one, user_moment_two)]

time: 127 us -> 126 us (level)
  no operation moved by 1% of the time
where the time goes in v6:
time: 126 us
  waiting for transfers between devices  43.9 us (35%)
  starting transfers between devices  37.6 us (30%)
  blocking collectives  23.6 us (19%)
  Pallas kernels  18.4 us (15%)
  between operations  1.4 us (1%)
    all_to_all x1, starting transfers between devices, on_device(): half = lax.all_to_all(shared, ('z_hi', 'y'), 0, 0)  20 us
    all_to_all x1, blocking collectives, on_device(): got = lax.all_to_all(both, ('z_hi', 'y'), 0, 0)  19.7 us
    all_to_all x1, waiting for transfers between devices, on_device(): new_low = lax.all_to_all(shared, ITEMS, 0, 0).reshape(-1, RANK)  15.8 us
    all_to_all x1, waiting for transfers between devices, on_device(): got = lax.all_to_all(sent, ITEMS, 0, 0)  15.8 us
    all_to_all x1, waiting for transfers between devices, on_device(): half = lax.all_to_all(shared, ('z_hi', 'y'), 0, 0)  11.3 us
    all_to_all x1, starting transfers between devices, on_device(): got = lax.all_to_all(sent, ITEMS, 0, 0)  9.78 us
    pallas_call x1, Pallas kernels, user_pass(): pl.pallas_call(user_kernel, out_shape=(jax.ShapeDtypeStruct((UBLK * EDGE,...  8.46 us
    pallas_call x1, Pallas kernels, item_pass(): pl.pallas_call(item_kernel, out_shape=(jax.ShapeDtypeStruct((ranks, share...  6.68 us
  transfers between devices with their start and end apart: 4, of which 4 were waited for; matrix products, arithmetic and copies ran while one was open for 0% of the time, Pallas kernels for 0%

profile of v6, /device:TPU:1, one launch (start us, length us, event | category | flops | bytes accessed | tf_op | source)
XLA Modules:
  0.0 125.6 jit_solution(11582327031193072474)
XLA Ops:
  0.6 1.4 %share_items.1 = bf16[24,32,128]{2,1,0:T(8,128)(2,1)} custom-call(f32[32,128]{1,0:T(8,128)} %items.1), custom_call_target="tpu_custom_call" | custom-call | tf_op jit(solution)/shard_map/share_items/pallas_call | solution.py:204
  2.0 20.0 %all-to-all-start = ((bf16[24,32,128]{2,1,0:T(8,128)(2,1)}), bf16[24,32,128]{2,1,0:T(8,128)(2,1)S(1)}, u32[]{:S(2)}, u32[]{:S(2)}) async-start(bf16[24,32,128]{2,1,0:T(8,128)(2,1)} %share_items.1), calls=%async_computation | async-start | bytes 393216 | tf_op jit(solution)/shard_map/all_to_all | solution.py:306
  22.7 11.3 %all-to-all-done = bf16[24,32,128]{2,1,0:T(8,128)(2,1)S(1)} async-done(((bf16[24,32,128]{2,1,0:T(8,128)(2,1)}), bf16[24,32,128]{2,1,0:T(8,128)(2,1)S(1)}, u32[]{:S(2)}, u32[]{:S(2)}) %all-to-all-start) | async-done | bytes 196640 | tf_op jit(solution)/shard_map/all_to_all | solution.py:306
  34.0 3.9 %all-gather = bf16[48,32,128]{2,1,0:T(8,128)(2,1)S(1)} all-gather(bf16[24,32,128]{2,1,0:T(8,128)(2,1)S(1)} %all-to-all-done), channel_id=2, replica_groups=mesh['z_hi'=3,'y'=8,'core'=2,'x'=4,'z_lo'=4] {'core'}, dimensions={0}, use_global_device_ids=true | all-gather | bytes 589824 | tf_op jit(solution)/shard_map/all_gather | solution.py:307
  37.9 8.5 %user_pass.1 = (bf16[2048,128]{1,0:T(8,128)(2,1)}, bf16[1536,128]{1,0:T(8,128)(2,1)S(1)}, s32[192]{0:T(256)S(1)}) custom-call(s32[128]{0:T(128)} %bitcast.13, s32[1]{0:T(128)} %bitcast.8.count, f32[2048,128]{1,0:T(8,128)} %parameter.1, bf16[2,24,32,128]{3,2,1,0:T(8,128)(2,1)S(1)} %bitcast.10, bf16[128,128,128]{2,1,0:T(8,128)(2,1)} %bitcast.11), custom_call_target="tpu_custom_call" | custom-call | tf_op jit(solution)/shard_map/user_pass/pallas_call | solution.py:215
  46.4 9.8 %all-to-all-start.1 = ((bf16[16,128,128]{2,1,0:T(8,128)(2,1)}), bf16[16,128,128]{2,1,0:T(8,128)(2,1)S(1)}, u32[]{:S(2)}, u32[]{:S(2)}) async-start(bf16[16,128,128]{2,1,0:T(8,128)(2,1)} %bitcast.5), calls=%async_computation.1 | async-start | bytes 1048576 | tf_op jit(solution)/shard_map/all_to_all | solution.py:312
  56.2 15.8 %all-to-all-done.1.got = bf16[16,128,128]{2,1,0:T(8,128)(2,1)S(1)} async-done(((bf16[16,128,128]{2,1,0:T(8,128)(2,1)}), bf16[16,128,128]{2,1,0:T(8,128)(2,1)S(1)}, u32[]{:S(2)}, u32[]{:S(2)}) %all-to-all-start.1) | async-done | bytes 524320 | tf_op jit(solution)/shard_map/all_to_all | solution.py:312
  71.9 1.8 %user_update.1 = (f32[128,128]{1,0:T(8,128)}, f32[128,128]{1,0:T(8,128)}, f32[128,128]{1,0:T(8,128)}, bf16[16,128,128]{2,1,0:T(8,128)(2,1)}) custom-call(s32[1]{0:T(128)} %bitcast.offset, bf16[16,128,128]{2,1,0:T(8,128)(2,1)S(1)} %all-to-all-done.1.got, f32[2048,128]{1,0:T(8,128)} %parameter.1, f32[2048,128]{1,0:T(8,128)} %first.1, f32[2048,128]{1,0:T(8,128)} %second.1), custom_call_target="tpu_custom_call" | custom-call | tf_op jit(solution)/shard_map/user_update/pallas_call | solution.py:270
  73.8 0.0 copy-start
  73.8 0.0 copy-start.1
  73.8 0.0 copy-start.2
  73.8 4.2 %all-to-all-start.2 = ((bf16[16,128,128]{2,1,0:T(8,128)(2,1)}), bf16[16,128,128]{2,1,0:T(8,128)(2,1)S(1)}, u32[]{:S(2)}, u32[]{:S(2)}) async-start(bf16[16,128,128]{2,1,0:T(8,128)(2,1)} %get-tuple-element.20), calls=%async_computation.2 | async-start | bytes 1048576 | tf_op jit(solution)/shard_map/all_to_all | solution.py:316
  78.1 15.8 %all-to-all-done.2 = bf16[16,128,128]{2,1,0:T(8,128)(2,1)S(1)} async-done(((bf16[16,128,128]{2,1,0:T(8,128)(2,1)}), bf16[16,128,128]{2,1,0:T(8,128)(2,1)S(1)}, u32[]{:S(2)}, u32[]{:S(2)}) %all-to-all-start.2) | async-done | bytes 524320 | tf_op jit(solution)/shard_map/all_to_all | solution.py:316
  93.8 6.7 %item_pass.1 = (f32[24,32,128]{2,1,0:T(8,128)S(1)}, bf16[24,32,128]{2,1,0:T(8,128)(2,1)S(1)}) custom-call(s32[1]{0:T(128)} %bitcast.6.core, s32[192]{0:T(256)S(1)} %get-tuple-element.19.places, bf16[2048,128]{1,0:T(8,128)(2,1)S(1)} %bitcast.9, bf16[1536,128]{1,0:T(8,128)(2,1)S(1)} %get-tuple-element.21.items, bf16[128,128,128]{2,1,0:T(8,128)(2,1)} %bitcast.12), custom_call_target="tpu_custom_call" | custom-call | tf_op jit(solution)/shard_map/item_pass/pallas_call | solution.py:244
  100.5 3.6 %collective-permute-start = (bf16[24,32,128]{2,1,0:T(8,128)(2,1)S(1)}, bf16[24,32,128]{2,1,0:T(8,128)(2,1)S(1)}, u32[]{:S(2)}, u32[]{:S(2)}) collective-permute-start(bf16[24,32,128]{2,1,0:T(8,128)(2,1)S(1)} %get-tuple-element.23), channel_id=1, source_target_pairs={{0,16},{16,0},{1,17},{17,1},{2,18},{18,2},{3,19},{19,3},{4,20},{20... | collective-permute-start | bytes 589832 | tf_op jit(solution)/shard_map/ppermute | solution.py:319
  104.1 1.0 collective-permute-done
  105.2 0.1 add_convert_fusion
  105.2 19.7 %all_to_all.20 = bf16[24,32,128]{2,1,0:T(8,128)(2,1)S(1)} all-to-all(bf16[24,32,128]{2,1,0:T(8,128)(2,1)S(1)} %add_convert_fusion), channel_id=1, replica_groups=mesh['z_hi'=3,'y'=8,'core'=2,'x'=4,'z_lo'=4] {'z_hi','y'}, dimensions={0} | all-to-all | bytes 393216 | tf_op jit(solution)/shard_map/all_to_all | solution.py:321
  124.9 0.0 copy-done
  124.9 0.0 copy-done.1
  124.9 0.0 copy-done.2
  125.0 0.6 multiply_subtract_fusion
  (1 shorter events, 0.0 us)
Async XLA Ops:
  2.0 31.9 %all-to-all-start = ((bf16[24,32,128]{2,1,0:T(8,128)(2,1)}), bf16[24,32,128]{2,1,0:T(8,128)(2,1)S(1)}, u32[]{:S(2)}, u32[]{:S(2)}) async-start(bf16[24,32,128]{2,1,0:T(8,128)(2,1)} %share_items.1), calls=%async_computation | async-start | bytes 393216 | tf_op jit(solution)/shard_map/all_to_all | solution.py:306
  46.4 25.6 %all-to-all-start.1 = ((bf16[16,128,128]{2,1,0:T(8,128)(2,1)}), bf16[16,128,128]{2,1,0:T(8,128)(2,1)S(1)}, u32[]{:S(2)}, u32[]{:S(2)}) async-start(bf16[16,128,128]{2,1,0:T(8,128)(2,1)} %bitcast.5), calls=%async_computation.1 | async-start | bytes 1048576 | tf_op jit(solution)/shard_map/all_to_all | solution.py:312
  73.8 51.1 %copy-start = (f32[32,128]{1,0:T(8,128)S(1)}, f32[32,128]{1,0:T(8,128)}, u32[]{:S(2)}) copy-start(f32[32,128]{1,0:T(8,128)} %items.1) | copy-start | bytes 49156
  73.8 51.1 %copy-start.1 = (f32[32,128]{1,0:T(8,128)S(1)}, f32[32,128]{1,0:T(8,128)}, u32[]{:S(2)}) copy-start(f32[32,128]{1,0:T(8,128)} %param.13) | copy-start | bytes 49156
  73.8 51.1 %copy-start.2 = (f32[32,128]{1,0:T(8,128)S(1)}, f32[32,128]{1,0:T(8,128)}, u32[]{:S(2)}) copy-start(f32[32,128]{1,0:T(8,128)} %param.14) | copy-start | bytes 49156
  73.8 20.0 %all-to-all-start.2 = ((bf16[16,128,128]{2,1,0:T(8,128)(2,1)}), bf16[16,128,128]{2,1,0:T(8,128)(2,1)S(1)}, u32[]{:S(2)}, u32[]{:S(2)}) async-start(bf16[16,128,128]{2,1,0:T(8,128)(2,1)} %get-tuple-element.20), calls=%async_computation.2 | async-start | bytes 1048576 | tf_op jit(solution)/shard_map/all_to_all | solution.py:316
  100.5 4.7 %collective-permute-start = (bf16[24,32,128]{2,1,0:T(8,128)(2,1)S(1)}, bf16[24,32,128]{2,1,0:T(8,128)(2,1)S(1)}, u32[]{:S(2)}, u32[]{:S(2)}) collective-permute-start(bf16[24,32,128]{2,1,0:T(8,128)(2,1)S(1)} %get-tuple-element.23), channel_id=1, source_target_pairs={{0,16},{16,0},{1,17},{17,1},{2,18},{18,2},{3,19},{19,3},{4,20},{20... | collective-permute-start | bytes 589832 | tf_op jit(solution)/shard_map/ppermute | solution.py:319
